TPU v7x, 32 devices: a whole 2x2x4 slice. The times are simulated.
32 devices in a mesh: batch: 8 (over z, x), blk: 4 (over y, core).
Axes of the slice: x: 2, y: 2, z: 4, core: 2. Of those that a mesh axis runs over, the one named last changes fastest.
Arguments:
- inputs: bfloat16 [8, 2048, 1024], P('batch', 'blk'), may hold values from -6 to 6
- ln1_gain: float32 [1024], replicated, may hold values from 0.1 to 1.9
- ln1_bias: float32 [1024], replicated, may hold values from -1 to 1
- w_qkv: bfloat16 [1024, 3072], replicated, may hold values from -0.1875 to 0.1875
- bias_q: float32 [1024], replicated, may hold values from -1.5 to 1.5
- bias_v: float32 [1024], replicated, may hold values from -0.25 to 0.25
- w_out: bfloat16 [1024, 1024], replicated, may hold values from -2 to 2
- bias_out: float32 [1024], replicated, may hold values from -1 to 1
- ln2_gain: float32 [1024], replicated, may hold values from 0.1 to 1.9
- ln2_bias: float32 [1024], replicated, may hold values from -1 to 1
- w_up: bfloat16 [1024, 4096], replicated, may hold values from -0.1875 to 0.1875
- bias_up: float32 [4096], replicated, may hold values from -1.5 to 1.5
- w_down: bfloat16 [4096, 1024], replicated, may hold values from -0.09375 to 0.09375
- bias_down: float32 [1024], replicated, may hold values from -2.5 to 2.5
- lengths: int32 [8, 2, 3], P('batch'), may hold values from 1 to 640, as said below
- cotangent: bfloat16 [8, 2048, 1024], P('batch', 'blk'), may hold values from -6 to 6
Outputs:
- result: bfloat16 [8, 2048, 1024], P('batch', 'blk')
- grad_inputs: float32 [8, 2048, 1024], P('batch', 'blk')
- grad_ln1_gain: float32 [1024], P('batch')
- grad_ln1_bias: float32 [1024], P('batch')
- grad_w_qkv: float32 [1024, 3072], P('batch')
- grad_bias_q: float32 [1024], P('batch')
- grad_bias_v: float32 [1024], P('batch')
- grad_w_out: float32 [1024, 1024], P('batch')
- grad_bias_out: float32 [1024], P('batch')
- grad_ln2_gain: float32 [1024], P('batch')
- grad_ln2_bias: float32 [1024], P('batch')
- grad_w_up: float32 [1024, 4096], P('batch')
- grad_bias_up: float32 [4096], P('batch')
- grad_w_down: float32 [4096, 1024], P('batch')
- grad_bias_down: float32 [1024], P('batch')
Inputs may be any that keep to these rules, and one draw needn't show every extreme that they name: lengths[r, u] gives utterance u of row r as (phonemes, prompt frames, target frames), packed in order from slot 0; phonemes number 1 to 128, prompt frames 1 to 256, target frames 1 to 640; slots after a row's last utterance are padding.
All inputs are finite; a program needn't handle non-finite values.
Results may differ from a plain program's by a relative error of at most 0.018.
Values may be sent and summed in bfloat16 or wider, within the bound.
No kernel may reach another device: no remote copies, remote signals or barrier semaphores. Data moves between devices by JAX's collectives and lax.ppermute only.
A program may use at most 192 MiB of HBM per device.

v0:
```python
import jax
import jax.numpy as jnp
from jax import lax
from jax.sharding import PartitionSpec as P

D = 1024
H = 16
HD = 64


epsilon = 1e-05


def layer_norm(values, gain_vec, shift_vec):
    center = values - jnp.mean(values, axis=-1, keepdims=True)
    spread = jnp.mean(center * center, axis=-1, keepdims=True)
    return center * lax.rsqrt(spread + epsilon) * gain_vec + shift_vec


def piece_index(lengths, positions):
    piece_ends = jnp.cumsum(lengths.reshape(lengths.shape[0], -1), axis=1)
    return jnp.sum((positions[:, :, None] >= piece_ends[:, None, :]).astype(jnp.int32), axis=2)


def visible(pos_query, piece_query, pos_key, piece_key, piece_count):
    both_live = (piece_query < piece_count) & (piece_key < piece_count)
    same_utt = piece_query // 3 == piece_key // 3
    seg_query = piece_query % 3
    seg_key = piece_key % 3
    in_order = (seg_key < seg_query) | (seg_key == seg_query) & (
        (seg_query < 2) | (pos_key <= pos_query)
    )
    return (pos_query == pos_key) | both_live & same_utt & in_order


def cross_dot(left_side, right_side):
    return lax.dot_general(
        left_side, right_side, (((0,), (0,)), ((), ())), preferred_element_type=jnp.float32
    )


def back_dot(gradient, weight):
    return lax.dot_general(
        gradient, weight, (((1,), (1,)), ((), ())), preferred_element_type=jnp.float32
    )


def shards(
    inputs,
    ln1_gain,
    ln1_bias,
    w_qkv,
    bias_q,
    bias_v,
    w_out,
    bias_out,
    ln2_gain,
    ln2_bias,
    w_up,
    bias_up,
    w_down,
    bias_down,
    lengths,
    cotangent,
):
    row_count, frame_count, _ = inputs.shape
    key_span = frame_count * lax.axis_size("blk")
    tokens = row_count * frame_count
    head_group = min(2, H)
    group_cols = head_group * HD
    group_count = H // head_group
    score_scale = HD ** (-0.5)
    piece_count = 3 * lengths.shape[1]
    local_pos = lax.axis_index("blk") * frame_count + jnp.arange(frame_count, dtype=jnp.int32)
    all_pos = jnp.arange(key_span, dtype=jnp.int32)
    piece_local = piece_index(lengths, local_pos[None, :])
    piece_all = piece_index(lengths, all_pos[None, :])
    allowed = visible(
        local_pos[None, :, None],
        piece_local[:, :, None],
        all_pos[None, None, :],
        piece_all[:, None, :],
        piece_count,
    )
    flat_in = inputs.reshape(tokens, D).astype(jnp.float32)
    normed_low = layer_norm(flat_in, ln1_gain, ln1_bias).astype(jnp.bfloat16)
    projected = jnp.dot(normed_low, w_qkv, preferred_element_type=jnp.float32)
    query_rows = (projected[:, :D] + bias_q).astype(jnp.bfloat16).reshape(row_count, frame_count, D)
    key_rows = projected[:, D : 2 * D].astype(jnp.bfloat16).reshape(row_count, frame_count, D)
    value_rows = (
        (projected[:, 2 * D :] + bias_v).astype(jnp.bfloat16).reshape(row_count, frame_count, D)
    )
    key_all, value_all = (
        lax.all_gather(key_rows, "blk", axis=1, tiled=True),
        lax.all_gather(value_rows, "blk", axis=1, tiled=True),
    )

    def head_slice(tensor, head_index):
        picked = lax.dynamic_slice_in_dim(tensor, head_index * group_cols, group_cols, 2)
        return picked.reshape(tensor.shape[0], tensor.shape[1], head_group, HD)

    def scores_of(query_part, key_part, mask):
        raw_scores = (
            jnp.einsum("rfgd,rlgd->rgfl", query_part, key_part, preferred_element_type=jnp.float32)
            * score_scale
        )
        return jnp.where(mask[:, None], raw_scores, -1e30)

    def forward_group(head_index, state_tuple):
        context, log_total = state_tuple
        scores = scores_of(
            head_slice(query_rows, head_index), head_slice(key_all, head_index), allowed
        )
        top_score = jnp.max(scores, axis=-1, keepdims=True)
        exponent = jnp.exp(scores - top_score)
        exp_total = jnp.sum(exponent, axis=-1, keepdims=True)
        weights = (exponent / exp_total).astype(jnp.bfloat16)
        context_part = jnp.einsum(
            "rgfl,rlgd->rfgd",
            weights,
            head_slice(value_all, head_index),
            preferred_element_type=jnp.float32,
        )
        context = lax.dynamic_update_slice_in_dim(
            context,
            context_part.reshape(row_count, frame_count, group_cols),
            head_index * group_cols,
            2,
        )
        log_total = lax.dynamic_update_slice_in_dim(
            log_total, (top_score + jnp.log(exp_total))[..., 0], head_index * head_group, 1
        )
        return (context, log_total)

    context, log_total = lax.fori_loop(
        0,
        group_count,
        forward_group,
        (
            jnp.zeros((row_count, frame_count, D), jnp.float32),
            jnp.zeros((row_count, H, frame_count), jnp.float32),
        ),
    )
    context_low = context.astype(jnp.bfloat16).reshape(tokens, D)
    middle = flat_in + (jnp.dot(context_low, w_out, preferred_element_type=jnp.float32) + bias_out)
    normed_two_low = layer_norm(middle, ln2_gain, ln2_bias).astype(jnp.bfloat16)
    hidden = jnp.dot(normed_two_low, w_up, preferred_element_type=jnp.float32) + bias_up
    active = jax.nn.gelu(hidden, approximate=False).astype(jnp.bfloat16)
    output = middle + (jnp.dot(active, w_down, preferred_element_type=jnp.float32) + bias_down)
    result = output.astype(jnp.bfloat16).reshape(row_count, frame_count, D)
    upstream = cotangent.reshape(tokens, D)
    upstream_f = upstream.astype(jnp.float32)
    grad_w_down = cross_dot(active, upstream)
    grad_bias_down = jnp.sum(upstream_f, axis=0)
    grad_active = back_dot(upstream, w_down)
    _, gelu_back = jax.vjp(lambda values: jax.nn.gelu(values, approximate=False), hidden)
    grad_hidden = gelu_back(grad_active)[0].astype(jnp.bfloat16)
    grad_w_up = cross_dot(normed_two_low, grad_hidden)
    grad_bias_up = jnp.sum(grad_hidden.astype(jnp.float32), axis=0)
    grad_normed_two = back_dot(grad_hidden, w_up)
    _, norm_back_two = jax.vjp(layer_norm, middle, ln2_gain, ln2_bias)
    grad_middle_norm, grad_ln2_gain, grad_ln2_bias = norm_back_two(grad_normed_two)
    grad_middle = upstream_f + grad_middle_norm
    grad_branch = grad_middle.astype(jnp.bfloat16)
    grad_w_out = cross_dot(context_low, grad_branch)
    grad_bias_out = jnp.sum(grad_branch.astype(jnp.float32), axis=0)
    grad_context = (
        back_dot(grad_branch, w_out).astype(jnp.bfloat16).reshape(row_count, frame_count, D)
    )
    key_back, value_back = (key_all, value_all)

    def score_grads(query_part, key_part, value_part, grad_part, log_block, mask, dot_block):
        prob_full = jnp.exp(scores_of(query_part, key_part, mask) - log_block)
        grad_weights = jnp.einsum(
            "rfgd,rlgd->rgfl", grad_part, value_part, preferred_element_type=jnp.float32
        )
        dot_block = jnp.sum(prob_full * grad_weights, axis=-1, keepdims=True)
        grad_scores = (prob_full * (grad_weights - dot_block)).astype(jnp.bfloat16)
        return (prob_full, grad_scores, dot_block)

    def backward_group(head_index, state_tuple):
        grad_query, grad_key, grad_value = state_tuple
        query_part = head_slice(query_rows, head_index)
        key_part = head_slice(key_back, head_index)
        grad_part = head_slice(grad_context, head_index)
        log_block = lax.dynamic_slice_in_dim(log_total, head_index * head_group, head_group, 1)[
            ..., None
        ]
        prob_full, grad_scores, _ = score_grads(
            query_part,
            key_part,
            head_slice(value_back, head_index),
            grad_part,
            log_block,
            allowed,
            None,
        )
        value_term = jnp.einsum(
            "rgfl,rfgd->rlgd",
            prob_full.astype(jnp.bfloat16),
            grad_part,
            preferred_element_type=jnp.float32,
        )
        query_term = (
            jnp.einsum("rgfl,rlgd->rfgd", grad_scores, key_part, preferred_element_type=jnp.float32)
            * score_scale
        )
        key_term = (
            jnp.einsum(
                "rgfl,rfgd->rlgd", grad_scores, query_part, preferred_element_type=jnp.float32
            )
            * score_scale
        )
        grad_query = lax.dynamic_update_slice_in_dim(
            grad_query,
            query_term.reshape(row_count, frame_count, group_cols),
            head_index * group_cols,
            2,
        )
        grad_key = lax.dynamic_update_slice_in_dim(
            grad_key, key_term.reshape(row_count, key_span, group_cols), head_index * group_cols, 2
        )
        grad_value = lax.dynamic_update_slice_in_dim(
            grad_value,
            value_term.reshape(row_count, key_span, group_cols),
            head_index * group_cols,
            2,
        )
        return (grad_query, grad_key, grad_value)

    grad_query, grad_key, grad_value = lax.fori_loop(
        0,
        group_count,
        backward_group,
        (
            jnp.zeros((row_count, frame_count, D), jnp.float32),
            jnp.zeros((row_count, key_span, D), jnp.float32),
            jnp.zeros((row_count, key_span, D), jnp.float32),
        ),
    )
    grad_key_own, grad_value_own = (
        lax.psum_scatter(
            grad_key.astype(jnp.bfloat16), "blk", scatter_dimension=1, tiled=True
        ).astype(jnp.float32),
        lax.psum_scatter(
            grad_value.astype(jnp.bfloat16), "blk", scatter_dimension=1, tiled=True
        ).astype(jnp.float32),
    )
    grad_qkv = jnp.concatenate(
        [
            grad_query.astype(jnp.bfloat16),
            grad_key_own.astype(jnp.bfloat16),
            grad_value_own.astype(jnp.bfloat16),
        ],
        axis=2,
    ).reshape(tokens, 3 * D)
    grad_w_qkv = cross_dot(normed_low, grad_qkv)
    grad_bias_q = jnp.sum(grad_qkv[:, :D].astype(jnp.float32), axis=0)
    grad_bias_v = jnp.sum(grad_qkv[:, 2 * D :].astype(jnp.float32), axis=0)
    grad_normed = back_dot(grad_qkv, w_qkv)
    _, norm_back_one = jax.vjp(layer_norm, flat_in, ln1_gain, ln1_bias)
    grad_input_norm, grad_ln1_gain, grad_ln1_bias = norm_back_one(grad_normed)
    grad_inputs = (grad_middle + grad_input_norm).reshape(row_count, frame_count, D)
    all_shards = (
        lax.psum_scatter(
            grad_ln1_gain.astype(jnp.bfloat16), "batch", scatter_dimension=0, tiled=True
        ).astype(jnp.float32),
        lax.psum_scatter(
            grad_ln1_bias.astype(jnp.bfloat16), "batch", scatter_dimension=0, tiled=True
        ).astype(jnp.float32),
        lax.psum_scatter(
            grad_w_qkv.astype(jnp.bfloat16), "batch", scatter_dimension=0, tiled=True
        ).astype(jnp.float32),
        lax.psum_scatter(
            grad_bias_q.astype(jnp.bfloat16), "batch", scatter_dimension=0, tiled=True
        ).astype(jnp.float32),
        lax.psum_scatter(
            grad_bias_v.astype(jnp.bfloat16), "batch", scatter_dimension=0, tiled=True
        ).astype(jnp.float32),
        lax.psum_scatter(
            grad_w_out.astype(jnp.bfloat16), "batch", scatter_dimension=0, tiled=True
        ).astype(jnp.float32),
        lax.psum_scatter(
            grad_bias_out.astype(jnp.bfloat16), "batch", scatter_dimension=0, tiled=True
        ).astype(jnp.float32),
        lax.psum_scatter(
            grad_w_up.astype(jnp.bfloat16), "batch", scatter_dimension=0, tiled=True
        ).astype(jnp.float32),
        lax.psum_scatter(
            grad_bias_up.astype(jnp.bfloat16), "batch", scatter_dimension=0, tiled=True
        ).astype(jnp.float32),
        lax.psum_scatter(
            grad_w_down.astype(jnp.bfloat16), "batch", scatter_dimension=0, tiled=True
        ).astype(jnp.float32),
        lax.psum_scatter(
            grad_bias_down.astype(jnp.bfloat16), "batch", scatter_dimension=0, tiled=True
        ).astype(jnp.float32),
        lax.psum_scatter(
            grad_ln2_gain.astype(jnp.bfloat16), "batch", scatter_dimension=0, tiled=True
        ).astype(jnp.float32),
        lax.psum_scatter(
            grad_ln2_bias.astype(jnp.bfloat16), "batch", scatter_dimension=0, tiled=True
        ).astype(jnp.float32),
    )
    summed = (
        lax.psum(all_shards[0].astype(jnp.bfloat16), "blk").astype(jnp.float32),
        lax.psum(all_shards[1].astype(jnp.bfloat16), "blk").astype(jnp.float32),
        lax.psum(all_shards[2].astype(jnp.bfloat16), "blk").astype(jnp.float32),
        lax.psum(all_shards[3].astype(jnp.bfloat16), "blk").astype(jnp.float32),
        lax.psum(all_shards[4].astype(jnp.bfloat16), "blk").astype(jnp.float32),
        lax.psum(all_shards[5].astype(jnp.bfloat16), "blk").astype(jnp.float32),
        lax.psum(all_shards[6].astype(jnp.bfloat16), "blk").astype(jnp.float32),
        lax.psum(all_shards[7].astype(jnp.bfloat16), "blk").astype(jnp.float32),
        lax.psum(all_shards[8].astype(jnp.bfloat16), "blk").astype(jnp.float32),
        lax.psum(all_shards[9].astype(jnp.bfloat16), "blk").astype(jnp.float32),
        lax.psum(all_shards[10].astype(jnp.bfloat16), "blk").astype(jnp.float32),
        lax.psum(all_shards[11].astype(jnp.bfloat16), "blk").astype(jnp.float32),
        lax.psum(all_shards[12].astype(jnp.bfloat16), "blk").astype(jnp.float32),
    )
    return (
        result,
        grad_inputs,
        summed[0],
        summed[1],
        summed[2],
        summed[3],
        summed[4],
        summed[5],
        summed[6],
        summed[11],
        summed[12],
        summed[7],
        summed[8],
        summed[9],
        summed[10],
    )


def solution(mesh):
    placed = (
        P("batch", "blk", None),
        P(),
        P(),
        P(),
        P(),
        P(),
        P(),
        P(),
        P(),
        P(),
        P(),
        P(),
        P(),
        P(),
        P("batch", None, None),
        P("batch", "blk", None),
    )
    return jax.shard_map(
        shards,
        mesh=mesh,
        in_specs=placed,
        out_specs=(
            P("batch", "blk", None),
            P("batch", "blk", None),
            P("batch"),
            P("batch"),
            P("batch", None),
            P("batch"),
            P("batch"),
            P("batch", None),
            P("batch"),
            P("batch"),
            P("batch"),
            P("batch", None),
            P("batch"),
            P("batch", None),
            P("batch"),
        ),
        check_vma=False,
    )
```

profile of v0, /device:TPU:0, one launch (start us, length us, event | category | flops | bytes accessed | tf_op | source)
XLA Modules:
  0.0 1234.7 jit_solution(13183961599949078790)
XLA Ops:
  11.1 6.1 fusion.58
  26.5 32.4 %all-gather.5.cloned.1.call-done = bf16[2048,1024]{1,0:T(8,128)(2,1)} async-done(((bf16[512,1024]{1,0:T(8,128)(2,1)}), bf16[2048,1024]{1,0:T(8,128)(2,1)}) %all-gather.5.cloned.1.call-update) | async-done | bytes 4194320 | tf_op jit(solution)/shard_map/all_gather | solution.py:95
  58.8 6.5 copy.45
  65.3 30.2 %all-gather.7.cloned.1.call-done = bf16[2048,1024]{1,0:T(8,128)(2,1)} async-done(((bf16[512,1024]{1,0:T(8,128)(2,1)}), bf16[2048,1024]{1,0:T(8,128)(2,1)}) %all-gather.7.cloned.1.call-update) | async-done | bytes 4194320 | tf_op jit(solution)/shard_map/all_gather | solution.py:94
  95.5 6.5 copy.47
  103.0 173.2 %while.34 = (s32[]{:T(128)}, bf16[1,512,1024]{1,2,0:T(8,128)(2,1)}, f32[1,16,512]{2,1,0:T(8,128)S(1)}, bf16[1,2048,1024]{1,2,0:T(8,128)(2,1)}, bf16[1,512,1024]{...) while((s32[]{:T(128)}, bf16[1,512,1024]{1,2,0:T(8,128)(2,1)}, ...), condition=%wide.region_8.9_spmd.clone, body=%wide.region_5.8_spmd.clone.sunk | while | flops 574618624 | bytes 66905404 | solution.py:135
  106.1 4.0 fusion.143
  117.8 6.2 fusion.146
  127.7 4.0 fusion.143
  139.4 6.2 fusion.146
  149.4 4.0 fusion.143
  161.1 6.2 fusion.146
  171.0 4.0 fusion.143
  182.7 6.2 fusion.146
  192.7 4.0 fusion.143
  204.4 6.2 fusion.146
  214.3 4.0 fusion.143
  226.0 6.2 fusion.146
  235.9 4.0 fusion.143
  247.7 6.2 fusion.146
  257.6 4.0 fusion.143
  269.3 6.2 fusion.146
  279.6 28.2 %multiply_convert_fusion.1 = (bf16[512,4096]{1,0:T(8,128)(2,1)}, f32[512,4096]{1,0:T(8,128)}, f32[512,4096]{1,0:T(8,128)}) fusion(f32[4096]{0:T(1024)S(1)} %copy-done.32, bf16[1024,4096]{1,0:T(8,128)(2,1)} %param.30, f32[512,1024]{1,0:T(8,128)S(1)} %get-tuple-element.606, f32[1024]{0:T(1024)S(1)} %copy-done.33, f32[1024]{0:T(1024)S(1)} %copy-done.29, ...), kind=kOutput, calls=%fused_computation.52 | convolution fusion | flops 4436000768 | bytes 31485952 | tf_op jit(solution)/shard_map/dot_general | solution.py:147
  307.8 13.9 %fusion.92 = (bf16[4096]{0:T(1024)(128)(2,1)}, bf16[512,4096]{1,0:T(8,128)(2,1)S(1)}) fusion(f32[512,4096]{1,0:T(8,128)} %get-tuple-element.589, bf16[4096,1024]{1,0:T(8,128)(2,1)} %param.32, bf16[1,512,1024]{2,1,0:T(8,128)(2,1)S(1)} %copy-done.7, f32[512,4096]{1,0:T(8,128)} %get-tuple-element.607, f32[4096]{0:T(1024)S(1)} %copy-done.32), kind=kOutput, calls=%fused_computation.164 | convolution fusion | flops 4328517632 | bytes 30433280 | tf_op jit(solution)/shard_map/dot_general | solution.py:43
  321.7 9.7 multiply_reduce_fusion.1
  341.7 219.5 %while.35 = (s32[]{:T(128)}, bf16[1,512,1024]{1,2,0:T(8,128)(2,1)}, bf16[1,2048,1024]{1,2,0:T(8,128)(2,1)}, bf16[1,2048,1024]{1,2,0:T(8,128)(2,1)}, bf16[1,2048,...) while((s32[]{:T(128)}, bf16[1,512,1024]{1,2,0:T(8,128)(2,1)}, ...), condition=%wide.region_15.16_spmd.clone, body=%wide.region_13.15_spmd.clone.sunk | while | flops 1386871808 | bytes 100849008 | solution.py:231
  343.7 4.5 fusion.157
  350.4 4.0 fusion.158
  354.4 5.6 multiply_reduce_fusion.5
  371.2 4.5 fusion.157
  377.9 4.0 fusion.158
  381.9 5.6 multiply_reduce_fusion.5
  398.7 4.5 fusion.157
  405.3 4.0 fusion.158
  409.4 5.6 multiply_reduce_fusion.5
  426.1 4.5 fusion.157
  432.8 4.0 fusion.158
  436.8 5.6 multiply_reduce_fusion.5
  453.6 4.5 fusion.157
  460.3 4.0 fusion.158
  464.3 5.6 multiply_reduce_fusion.5
  481.0 4.5 fusion.157
  487.7 4.0 fusion.158
  491.7 5.6 multiply_reduce_fusion.5
  508.4 4.5 fusion.157
  519.1 5.6 multiply_reduce_fusion.5
  535.8 4.5 fusion.157
  546.5 5.6 multiply_reduce_fusion.5
  561.9 4.3 convolution_convert_fusion.3
  566.2 9.5 convolution_convert_fusion.1
  575.8 9.0 convolution_convert_fusion
  584.9 21.0 %reduce-scatter.7.cloned.1.call-done = bf16[1,512,1024]{1,2,0:T(8,128)(2,1)} async-done(((bf16[1,2048,1024]{1,2,0:T(8,128)(2,1)}), bf16[1,512,1024]{1,2,0:T(8,128)(2,1)}) %reduce-scatter.7.cloned.1.call-update) | async-done | bytes 1048592 | tf_op jit(solution)/shard_map/reduce_scatter | solution.py:242
  605.9 47.1 %reduce-scatter.9.cloned.1.call-done = bf16[1,512,1024]{1,2,0:T(8,128)(2,1)} async-done(((bf16[1,2048,1024]{1,2,0:T(8,128)(2,1)}), bf16[1,512,1024]{1,2,0:T(8,128)(2,1)}) %reduce-scatter.9.cloned.1.call-update) | async-done | bytes 1048592 | tf_op jit(solution)/shard_map/reduce_scatter | solution.py:245
  653.0 8.3 convolution_convert_fusion.2
  663.9 10.8 fusion.53
  674.7 8.2 fusion.86
  682.9 41.8 %reduce-scatter.13.cloned.1.call-done = bf16[128,1024]{1,0:T(8,128)(2,1)} async-done(((bf16[1024,1024]{1,0:T(8,128)(2,1)}), bf16[128,1024]{1,0:T(8,128)(2,1)}) %reduce-scatter.13.cloned.1.call-update) | async-done | bytes 262160 | tf_op jit(solution)/shard_map/reduce_scatter | solution.py:280
  724.7 151.5 %reduce-scatter.15.cloned.1.call-done = bf16[128,4096]{1,0:T(8,128)(2,1)} async-done(((bf16[1024,4096]{1,0:T(8,128)(2,1)}), bf16[128,4096]{1,0:T(8,128)(2,1)}) %reduce-scatter.15.cloned.1.call-update) | async-done | bytes 1048592 | tf_op jit(solution)/shard_map/reduce_scatter | solution.py:286
  876.3 152.1 %reduce-scatter.17.cloned.1.call-done = bf16[512,1024]{1,0:T(8,128)(2,1)} async-done(((bf16[4096,1024]{1,0:T(8,128)(2,1)}), bf16[512,1024]{1,0:T(8,128)(2,1)}) %reduce-scatter.17.cloned.1.call-update) | async-done | bytes 1048592 | tf_op jit(solution)/shard_map/reduce_scatter | solution.py:292
  1028.3 120.6 %reduce-scatter.11.cloned.1.call-done = bf16[128,3072]{1,0:T(8,128)(2,1)} async-done(((bf16[1024,3072]{1,0:T(8,128)(2,1)}), bf16[128,3072]{1,0:T(8,128)(2,1)}) %reduce-scatter.11.cloned.1.call-update) | async-done | bytes 786448 | tf_op jit(solution)/shard_map/reduce_scatter | solution.py:271
  1152.3 35.3 %all-reduce.9 = (bf16[1024]{0:T(1024)(128)(2,1)S(1)}, bf16[1024]{0:T(1024)(128)(2,1)S(1)}, bf16[1024]{0:T(1024)(128)(2,1)S(1)}, bf16[1024]{0:T(1024)(128)(2,1)S(...) all-reduce(bf16[1024]{0:T(1024)(128)(2,1)S(1)} %get-tuple-element.4, ...), channel_id=6, replica_groups=mesh['batch'=8,'blk'=4] {'batch'}, use_global_device_ids=true, to_apply=%region_21.22.clone | all-reduce | flops 12288 | bytes 49152
  1188.3 5.7 all-reduce.10
  1198.7 4.5 add_bitcast_fusion
  1203.2 16.6 %all-reduce.14.cloned.1.call-done = (bf16[128,3072]{1,0:T(8,128)(2,1)}, bf16[128,1024]{1,0:T(8,128)(2,1)}, bf16[128,4096]{1,0:T(8,128)(2,1)}, bf16[512,1024]{1,0:T(8,128)(2,1)}) async-done(((bf16[128,3072]{1,0:T(8,128)(2,1)}, bf16[128,1024]{1,0:T(8,128)(2,1)}, bf16[128,4096]{1,0:T(8,128)(2,1)}, bf16[512,1024]{1,0:T(8,128)(2,1)}), (bf16[128,3072]{1,0:T(8,128)(2,1)}, bf16[128,1024]{1,0:T(8,128)(2,1)}, ...) | async-done | bytes 3145744 | tf_op jit(solution)/shard_map/psum | solution.py:308
  (355 shorter events, 250.2 us)
Async XLA Ops:
  7.2 269.0 %copy-start = (bf16[1024,1024]{1,0:T(8,128)(2,1)S(1)}, bf16[1024,1024]{1,0:T(8,128)(2,1)}, u32[]{:S(2)}) copy-start(bf16[1024,1024]{1,0:T(8,128)(2,1)} %param.26) | copy-start | bytes 6291460
  7.2 51.6 %all-gather.5.cloned.1.call-start = ((), (), s32[]{:S(2)}) async-start(), calls=%async_computation.12 | async-start | bytes 5242880 | tf_op jit(solution)/shard_map/all_gather | solution.py:95
  8.8 8.4 copy-start.16
  11.1 6.1 copy-start.22
  11.1 8.8 copy-start.27
  11.1 8.8 copy-start.28
  17.2 2.7 copy-start.9
  21.5 4.4 copy-start.36
  21.5 74.0 %all-gather.7.cloned.1.call-start = ((), (), s32[]{:S(2)}) async-start(), calls=%async_computation.13 | async-start | bytes 5242880 | tf_op jit(solution)/shard_map/all_gather | solution.py:94
  24.3 581.6 %reduce-scatter.7.cloned.1.call-start = ((), (), s32[]{:S(2)}) async-start(), calls=%async_computation.6 | async-start | bytes 5242880 | tf_op jit(solution)/shard_map/reduce_scatter | solution.py:242
  103.0 173.2 %copy-start.15 = (f32[1024]{0:T(1024)S(1)}, f32[1024]{0:T(1024)}, u32[]{:S(2)}) copy-start(f32[1024]{0:T(1024)} %param.27) | copy-start | bytes 12292
  112.1 3.2 copy-start.2
  133.7 3.2 copy-start.2
  155.4 3.2 copy-start.2
  177.0 3.2 copy-start.2
  198.7 3.2 copy-start.2
  220.3 3.2 copy-start.2
  242.0 3.2 copy-start.2
  263.6 3.2 copy-start.2
  276.2 3.3 copy-start.29
  276.2 3.3 copy-start.32
  276.2 3.3 copy-start.33
  279.2 52.3 %copy-start.5 = (f32[512,1024]{1,0:T(8,128)}, f32[512,1024]{1,0:T(8,128)S(1)}, u32[]{:S(2)}) copy-start(f32[512,1024]{1,0:T(8,128)S(1)} %get-tuple-element.606) | copy-start | bytes 6291460
  279.6 28.2 %copy-start.7 = (bf16[1,512,1024]{2,1,0:T(8,128)(2,1)S(1)}, bf16[1,512,1024]{2,1,0:T(8,128)(2,1)}, u32[]{:S(2)}) copy-start(bf16[1,512,1024]{2,1,0:T(8,128)(2,1)} %param.35) | copy-start | bytes 3145732
  321.7 9.8 copy-start.38
  332.1 3.5 copy-start.4
  332.2 3.5 copy-start.18
  333.4 2.3 copy-start.10
  350.4 9.7 slice-start
  354.4 5.6 slice-start.1
  377.8 9.7 slice-start
  381.9 5.6 slice-start.1
  405.3 9.7 slice-start
  409.4 5.6 slice-start.1
  432.8 9.7 slice-start
  436.8 5.6 slice-start.1
  460.3 9.7 slice-start
  464.3 5.6 slice-start.1
  487.7 9.7 slice-start
  491.7 5.6 slice-start.1
  515.1 9.7 slice-start
  519.1 5.6 slice-start.1
  542.5 9.7 slice-start
  546.5 5.6 slice-start.1
  561.2 91.7 %reduce-scatter.9.cloned.1.call-start = ((), (), s32[]{:S(2)}) async-start(), calls=%async_computation.7 | async-start | bytes 5242880 | tf_op jit(solution)/shard_map/reduce_scatter | solution.py:245
  561.8 4.4 copy-start.6
  561.8 162.9 %reduce-scatter.13.cloned.1.call-start = ((), (), s32[]{:S(2)}) async-start(), calls=%async_computation.9 | async-start | bytes 2359296 | tf_op jit(solution)/shard_map/reduce_scatter | solution.py:280
  566.2 310.1 %reduce-scatter.15.cloned.1.call-start = ((), (), s32[]{:S(2)}) async-start(), calls=%async_computation.10 | async-start | bytes 9437184 | tf_op jit(solution)/shard_map/reduce_scatter | solution.py:286
  575.8 452.5 %reduce-scatter.17.cloned.1.call-start = ((), (), s32[]{:S(2)}) async-start(), calls=%async_computation.11 | async-start | bytes 9437184 | tf_op jit(solution)/shard_map/reduce_scatter | solution.py:292
  584.8 68.1 %copy-start.3 = (bf16[1,512,1024]{2,1,0:T(8,128)(2,1)S(1)}, bf16[1,512,1024]{2,1,0:T(8,128)(2,1)}, u32[]{:S(2)}) copy-start(bf16[1,512,1024]{2,1,0:T(8,128)(2,1)} %param.20) | copy-start | bytes 3145732
  584.8 68.1 %copy-start.17 = (f32[512]{0:T(512)S(1)}, f32[512]{0:T(512)}, u32[]{:S(2)}) copy-start(f32[512]{0:T(512)} %copy-done.16) | copy-start | bytes 6148
  584.9 68.1 %copy-start.23 = (f32[512]{0:T(512)S(1)}, f32[512]{0:T(512)}, u32[]{:S(2)}) copy-start(f32[512]{0:T(512)} %copy-done.22) | copy-start | bytes 6148
  584.9 68.1 %copy-start.24 = (f32[1024]{0:T(1024)S(1)}, f32[1024]{0:T(1024)}, u32[]{:S(2)}) copy-start(f32[1024]{0:T(1024)} %param.21) | copy-start | bytes 12292
  584.9 68.1 %copy-start.34 = (f32[1024]{0:T(1024)S(1)}, f32[1024]{0:T(1024)}, u32[]{:S(2)}) copy-start(f32[1024]{0:T(1024)} %param.22) | copy-start | bytes 12292
  584.9 564.0 %reduce-scatter.11.cloned.1.call-start = ((), (), s32[]{:S(2)}) async-start(), calls=%async_computation.8 | async-start | bytes 7077888 | tf_op jit(solution)/shard_map/reduce_scatter | solution.py:271
  661.3 2.5 copy-start.35
  661.4 558.5 %all-reduce.14.cloned.1.call-start = ((), (), s32[]{:S(2)}) async-start(), calls=%async_computation.14 | async-start | bytes 6291456 | tf_op jit(solution)/shard_map/psum | solution.py:308
  663.9 10.8 copy-start.11
  663.9 10.8 copy-start.12
  1149.0 2.3 copy-start.8
  1150.8 47.9 %copy-start.19 = (f32[512]{0:T(512)S(1)}, f32[512]{0:T(512)}, u32[]{:S(2)}) copy-start(f32[512]{0:T(512)} %copy-done.18) | copy-start | bytes 6148
  1219.8 5.7 copy-start.13
  1219.8 7.9 copy-start.1
  1219.8 7.0 copy-start.14
  (7 other events, 9.4 us)
Sparse Core Ops, SparseCore 0:
  21.6 37.1 all-gather.4
  61.0 34.4 all-gather.6
  561.4 44.4 reduce-scatter.6
  608.4 44.4 reduce-scatter.8
  656.9 67.7 reduce-scatter.12
  728.2 147.9 reduce-scatter.14
  880.3 147.9 reduce-scatter.16
  1031.9 116.9 reduce-scatter.10
  1151.5 68.2 all-reduce.13
where the time goes:
time: 1240 us; the launch traced here: 1230 us
  waiting for transfers between devices  614 us (50%)
  matrix products  297 us (24%)
  other arithmetic  133 us (11%)
  local copies, waits for them, and re-layouts  132 us (11%)
  blocking collectives  41 us (3%)
  between operations  16 us (1%)
    reduce_scatter x1, waiting for transfers between devices, shards(): lax.psum_scatter(grad_w_down.astype(jnp.bfloat16), 'batch', scatter_dimen...  152 us
    reduce_scatter x1, waiting for transfers between devices, shards(): lax.psum_scatter(grad_w_up.astype(jnp.bfloat16), 'batch', scatter_dimensi...  152 us
    reduce_scatter x1, waiting for transfers between devices, shards(): lax.psum_scatter(grad_w_qkv.astype(jnp.bfloat16), 'batch', scatter_dimens...  121 us
    broadcast_in_dim x16, other arithmetic, scores_of(): return jnp.where(mask[:, None], raw_scores, -1e+30)  64.6 us
    dynamic_slice x56, local copies, waits for them, and re-layouts, head_slice(): lax.dynamic_slice_in_dim(tensor, head_index * group_cols, group_cols, 2)  57 us
    dot_general x16, matrix products, scores_of(): jnp.einsum('rfgd,rlgd->rgfl', query_part, key_part, preferred_element_typ...  51.8 us
    dot_general x8, matrix products, forward_group(): jnp.einsum('rgfl,rlgd->rfgd', weights, head_slice(value_all, head_index),...  49.8 us
    reduce_scatter x1, waiting for transfers between devices, shards(): lax.psum_scatter(grad_value.astype(jnp.bfloat16), 'blk', scatter_dimensio...  47.1 us
  transfers between devices with their start and end apart: 9, of which 9 were waited for; matrix products, arithmetic and copies ran while one was open for 6% of the time, Pallas kernels for 0%

commit v1 on v0

v1 whole, which is shorter than its diff:
```python
import functools

import jax
import jax.numpy as jnp
from jax import lax
from jax.experimental import pallas as pl
from jax.experimental.pallas import tpu as pltpu
from jax.sharding import Mesh
from jax.sharding import PartitionSpec as P

D = 1024
H = 16
HD = 64
EPS = 1e-05
NEG = -1e30
BF = jnp.bfloat16
F32 = jnp.float32


def layer_norm(values, gain_vec, shift_vec):
    center = values - jnp.mean(values, axis=-1, keepdims=True)
    spread = jnp.mean(center * center, axis=-1, keepdims=True)
    return center * lax.rsqrt(spread + EPS) * gain_vec + shift_vec


def dot(a, b):
    return jnp.dot(a, b, preferred_element_type=F32)


def dot_tn(a, b):
    return lax.dot_general(a, b, (((0,), (0,)), ((), ())), preferred_element_type=F32)


def dot_nt(a, b):
    return lax.dot_general(a, b, (((1,), (1,)), ((), ())), preferred_element_type=F32)


def half(a, h):
    a = a[:, (h // 2) * 2 * HD : (h // 2 + 1) * 2 * HD]
    lane = lax.broadcasted_iota(jnp.int32, a.shape, 1)
    zero = jnp.zeros_like(a)
    return jnp.where(lane < HD, a, zero) if h % 2 == 0 else jnp.where(lane < HD, zero, a)


def pair(a, h):
    return a[:, (h // 2) * 2 * HD : (h // 2 + 1) * 2 * HD]


def fwd_kernel(T, HG, lst, cnt, base, q_ref, k_ref, v_ref, lo_ref, hi_ref, ctx_ref, lse_ref):
    nq = q_ref.shape[0] // T
    row = lax.broadcasted_iota(jnp.int32, (T, T), 0)

    @pl.loop(0, nq)
    def _(qt):
        at = pl.ds(pl.multiple_of(qt * T, T), T)
        q = q_ref[at, :]
        qh = [half(q, h) for h in range(HG)]
        lo, hi = lo_ref[:, at], hi_ref[:, at]

        def body(n, carry):
            t = lst[qt, n]
            ks = pl.ds(pl.multiple_of(t * T, T), T)
            k, v = k_ref[ks, :], v_ref[ks, :].T
            vis = (row >= lo - base[t]) & (row < hi - base[t])
            raw = [dot_nt(pair(k, h), qh[h]) for h in range(HG)]
            out = []
            for h in range(HG):
                m, l, acc = carry[h]
                s = jnp.where(vis, raw[h], NEG)
                mn = jnp.maximum(m, jnp.max(s, axis=0, keepdims=True))
                a = jnp.exp(m - mn)
                p = jnp.exp(s - mn)
                l = a * l + jnp.sum(p, axis=0, keepdims=True)
                acc = acc * a + dot(v[h * HD : (h + 1) * HD, :], p.astype(BF))
                out.append((mn, l, acc))
            return tuple(out)

        one = (jnp.full((1, T), NEG, F32), jnp.zeros((1, T), F32), jnp.zeros((HD, T), F32))
        res = lax.fori_loop(0, cnt[qt], body, (one,) * HG)
        ctx_ref[at, :] = jnp.concatenate([r[2] / r[1] for r in res], axis=0).T.astype(BF)
        lse_ref[:, at] = jnp.concatenate([r[0] + jnp.log(r[1]) for r in res], axis=0)


def bwd_kernel(T, HG, lst, cnt, base, q_ref, k_ref, v_ref, ctx_ref, do_ref, lse_ref, lo_ref, hi_ref, out_ref, dqt, dl):
    n_tiles = q_ref.shape[0] // T
    W = HG * HD
    row = lax.broadcasted_iota(jnp.int32, (T, T), 0)
    lane = lax.broadcasted_iota(jnp.int32, (T, 2 * HD), 1)
    dqt[...] = jnp.zeros_like(dqt)

    @pl.loop(0, n_tiles)
    def _(t):
        at = pl.ds(pl.multiple_of(t * T, T), T)
        prod = (do_ref[at, :].astype(F32) * ctx_ref[at, :].astype(F32)).T
        dl[:, at] = jnp.concatenate([jnp.sum(prod[h * HD : (h + 1) * HD], axis=0, keepdims=True) for h in range(HG)], axis=0)

    @pl.loop(0, n_tiles)
    def _(kt):
        ks = pl.ds(pl.multiple_of(kt * T, T), T)
        k, v = k_ref[ks, :], v_ref[ks, :]
        kT = k.T
        kh, vh = [half(k, h) for h in range(HG)], [half(v, h) for h in range(HG)]

        def body(n, carry):
            at = pl.ds(pl.multiple_of(lst[kt, n] * T, T), T)
            q, do = q_ref[at, :], do_ref[at, :]
            vis = (row >= lo_ref[:, at] - base[kt]) & (row < hi_ref[:, at] - base[kt])
            raw = [dot_nt(kh[h], pair(q, h)) for h in range(HG)]
            dps = [dot_nt(vh[h], pair(do, h)) for h in range(HG)]
            out = []
            for h in range(HG):
                p = jnp.exp(jnp.where(vis, raw[h], NEG) - lse_ref[h : h + 1, at])
                ds = (p * (dps[h] - dl[h : h + 1, at])).astype(BF)
                out.append((carry[h][0] + dot(ds, pair(q, h)), carry[h][1] + dot(p.astype(BF), pair(do, h))))
                dqt[h * HD : (h + 1) * HD, at] += dot(kT[h * HD : (h + 1) * HD, :], ds)
            return tuple(out)

        one = (jnp.zeros((T, 2 * HD), F32), jnp.zeros((T, 2 * HD), F32))
        res = lax.fori_loop(0, cnt[kt], body, (one,) * HG)
        for p in range(HG // 2):
            cols = slice(p * 2 * HD, (p + 1) * 2 * HD)
            a, b = res[2 * p], res[2 * p + 1]
            out_ref[ks, W + cols.start : W + cols.stop] = jnp.where(lane < HD, a[0], b[0]).astype(BF)
            out_ref[ks, 2 * W + cols.start : 2 * W + cols.stop] = jnp.where(lane < HD, a[1], b[1]).astype(BF)

    @pl.loop(0, n_tiles)
    def _(t):
        at = pl.ds(pl.multiple_of(t * T, T), T)
        out_ref[at, :W] = (dqt[:, at].T * HD**-0.5).astype(BF)


def attend(kernel, scalars, ins, outs, scratch, flops):
    def spec(shape, cols):
        if cols is None:
            return pl.BlockSpec(shape, lambda i, *_: (0,) * len(shape))
        return pl.BlockSpec((shape[0], cols[0]), lambda i, *_: (0, cols[1]))

    size = sum(a.size * a.dtype.itemsize for a, _ in ins) + sum(o.size * o.dtype.itemsize for o in outs)
    return pl.pallas_call(
        kernel,
        out_shape=outs,
        grid_spec=pltpu.PrefetchScalarGridSpec(
            num_scalar_prefetch=len(scalars),
            grid=(1,),
            in_specs=[spec(a.shape, cols) for a, cols in ins],
            out_specs=[spec(o.shape, None) for o in outs],
            scratch_shapes=scratch,
        ),
        compiler_params=pltpu.CompilerParams(vmem_limit_bytes=40 << 20),
        cost_estimate=pl.CostEstimate(flops=flops, bytes_accessed=size, transcendentals=0),
    )(*scalars, *[a for a, _ in ins])


def tile_list(active):
    m = active.shape[1]
    hit = active.astype(jnp.int32)
    upto = jnp.tril(jnp.ones((m, m), jnp.int32))
    rank = jnp.sum(hit[:, None, :] * upto[None], axis=2) - 1
    ids = jnp.arange(m, dtype=jnp.int32)
    here = (rank[:, :, None] == ids[None, None, :]) & active[:, :, None]
    return jnp.sum(jnp.where(here, ids[None, :, None], 0), axis=1), jnp.sum(hit, axis=1)


def after(vals, deps):
    return lax.optimization_barrier((vals, deps))[0]


def shards(Z, X, Y, inputs, ln1_gain, ln1_bias, w_qkv, bias_q, bias_v, w_out, bias_out, ln2_gain, ln2_bias,
           w_up, bias_up, w_down, bias_down, lengths, cotangent):
    F = inputs.shape[1]
    K = 2 * Y
    S = F * K
    T = min(256, F)
    W = D // K
    HG = H // K
    B = Z * X
    zi, xi, y, c = (lax.axis_index(n) for n in ("z", "x", "y", "c"))
    group = y * 2 + c
    sds = jax.ShapeDtypeStruct

    def shift(v, axis, n, s):
        return lax.ppermute(v, axis, [(i, (i + s) % n) for i in range(n)])

    def mate(v):
        return lax.ppermute(v, "c", [(0, 1), (1, 0)])

    rel = [(s, d) for s in range(Y) for d in range(2)]

    def hop(v, s, d):
        pairs = [(yy * 2 + cc, ((yy + s) % Y) * 2 + (cc ^ d)) for yy in range(Y) for cc in range(2)]
        return lax.ppermute(v, ("y", "c"), pairs)

    def flip(d):
        return c if d == 0 else 1 - c

    blocks = jnp.stack([((y - s) % Y) * 2 + flip(d) for s, d in rel])
    ends = jnp.cumsum(lengths.reshape(-1))
    pos = (blocks[:, None] * F + jnp.arange(F, dtype=jnp.int32)[None]).reshape(1, S)
    piece = jnp.sum((pos >= ends[:, None]).astype(jnp.int32), axis=0, keepdims=True)
    pieces = ends.shape[0]
    starts = jnp.concatenate([jnp.zeros((1,), ends.dtype), ends[:-1]])

    def look(table, idx):
        return jnp.sum(jnp.where(idx == jnp.arange(pieces)[:, None], table[:, None], 0), axis=0, keepdims=True)

    pad = piece >= pieces
    lo = jnp.where(pad, pos, look(starts, (piece // 3) * 3)).astype(jnp.int32)
    hi = jnp.where(pad | (piece % 3 == 2), pos + 1, look(ends, piece)).astype(jnp.int32)
    base = pos[0, ::T].astype(jnp.int32)
    qlo = jnp.min(lo.reshape(S // T, T), axis=1)
    qhi = jnp.max(hi.reshape(S // T, T), axis=1)
    active = (base[None, :] < qhi[:, None]) & (base[None, :] + T > qlo[:, None])
    lst_q, cnt_q = tile_list(active)
    lst_k, cnt_k = tile_list(active.T)

    x_own = inputs.reshape(F, D)
    up = cotangent.reshape(F, D)
    flat_in = x_own.astype(F32)
    h1 = layer_norm(flat_in, ln1_gain, ln1_bias).astype(BF)
    got = [h1, mate(h1)]
    far = [shift(h1, "y", Y, s) for s in range(1, Y)]

    def cols_of(w, g):
        return [lax.dynamic_slice_in_dim(w, part * D + g * W, W, w.ndim - 1) for part in range(3)]

    w_g = jnp.concatenate(cols_of(w_qkv, group), axis=1)
    b_g = jnp.concatenate([lax.dynamic_slice_in_dim(bias_q, group * W, W, 0), jnp.zeros((W,), F32),
                           lax.dynamic_slice_in_dim(bias_v, group * W, W, 0)])
    sc_g = jnp.where(jnp.arange(3 * W) < W, HD**-0.5, 1.0).astype(BF)
    dg = dot_nt(after(up, h1), w_down).astype(BF)
    for r in far:
        got += [r, mate(r)]
    h_all = jnp.concatenate(got, axis=0)
    h_all, dg = lax.optimization_barrier((h_all, dg))
    qkv = (dot(h_all, w_g) + b_g).astype(BF) * sc_g
    lse_shape = sds((HG, S), F32)
    dense = S * S * W * 2 // 4
    ctx_g, lse = attend(
        functools.partial(fwd_kernel, T, HG), (lst_q, cnt_q, base),
        [(qkv, (W, 0)), (qkv, (W, 1)), (qkv, (W, 2)), (lo, None), (hi, None)],
        [sds((S, W), BF), lse_shape], [], 2 * dense)

    mine = [ctx_g[:F]] + [hop(ctx_g[(2 * s + d) * F : (2 * s + d + 1) * F], -s, d) for s, d in rel[1:]]
    mine = jnp.stack(mine)
    ctx = jnp.concatenate(
        [lax.dynamic_index_in_dim(mine, ((yy - y) % Y) * 2 + (cc ^ c), 0, keepdims=False)
         for yy in range(Y) for cc in range(2)], axis=1)
    middle = flat_in + (dot(ctx, w_out) + bias_out)
    h2 = layer_norm(middle, ln2_gain, ln2_bias).astype(BF)
    hidden = dot(h2, w_up) + bias_up
    act, gelu_back = jax.vjp(lambda t: jax.nn.gelu(t, approximate=False), hidden)
    act = act.astype(BF)
    du = gelu_back(dg.astype(F32))[0].astype(BF)

    def scatter(parts, axis, n, me):
        sent = [shift(lax.dynamic_index_in_dim(parts, (me + s) % n, 0, keepdims=False), axis, n, s) for s in range(1, n)]
        own = lax.dynamic_index_in_dim(parts, me, 0, keepdims=False).astype(F32)
        return sum((r.astype(F32) for r in sent), own).astype(BF)

    def give_c(a, b):
        n = b.shape[1] // 2
        return dot_tn(a, lax.dynamic_slice_in_dim(b, (1 - c) * n, n, 1)).astype(BF)

    def keep_c(a, b, got):
        n = b.shape[1] // 2
        return (dot_tn(a, lax.dynamic_slice_in_dim(b, c * n, n, 1)) + got.astype(F32)).astype(BF)

    def blocks_of(g):
        return g.reshape(Z, X, g.shape[0] // B, g.shape[1])

    def over_y(g):
        n = g.shape[-1] // Y
        return scatter(jnp.stack([g[..., i * n : (i + 1) * n] for i in range(Y)]), "y", Y, y)

    def over_x(g):
        return scatter(jnp.moveaxis(g, 1, 0), "x", X, xi)[:, None]

    def over_z(g):
        return scatter(g, "z", Z, zi)[None]

    def everywhere(g):
        two = jnp.stack([g, mate(g)])
        all_ = jnp.concatenate([two] + [shift(two, "y", Y, s) for s in range(1, Y)])
        return [[lax.dynamic_index_in_dim(all_, ((y - yy) % Y) * 2 + (cc ^ c), 0, keepdims=False) for cc in range(2)]
                for yy in range(Y)]

    def spread(g):
        e = everywhere(g)
        return jnp.concatenate([e[yy][cc] for cc in range(2) for yy in range(Y)], axis=1).astype(F32)

    down_give = give_c(act, up)
    down_got = mate(down_give)
    dh2 = dot_nt(after(du, down_give), w_up)
    _, norm_back_two = jax.vjp(layer_norm, middle, ln2_gain, ln2_bias)
    dmid, g_ln2g, g_ln2b = norm_back_two(dh2)
    dy1 = up.astype(F32) + dmid
    da = dy1.astype(BF)
    dctx = dot_nt(da, w_out).astype(BF)

    def heads_of(s, d):
        return lax.dynamic_slice_in_dim(dctx, (((y + s) % Y) * 2 + flip(d)) * W, W, 1)

    do_g = jnp.concatenate([heads_of(0, 0)] + [hop(heads_of(s, d), s, d) for s, d in rel[1:]], axis=0)

    act, up_, h2, du, ctx_ = after((act, up, h2, du, ctx), dctx)
    h_down = keep_c(act, up_, down_got)
    up_give = give_c(h2, du)
    up_got = mate(up_give)
    out_give = give_c(ctx_, da)
    out_got = mate(out_give)
    h_out = keep_c(ctx_, da, out_got)
    h_up = keep_c(h2, du, up_got)
    result = (middle + (dot(act, w_down) + bias_down)).astype(BF)
    one = jnp.concatenate([blocks_of(h_down).reshape(Z, X, -1, D // 2), blocks_of(h_out)], axis=2)
    two = blocks_of(h_up)
    do_g = after(do_g, (result, h_up, h_out))

    (dqkv,) = attend(
        functools.partial(bwd_kernel, T, HG), (lst_k, cnt_k, base),
        [(qkv, (W, 0)), (qkv, (W, 1)), (qkv, (W, 2)), (ctx_g, None), (do_g, None), (lse, None), (lo, None), (hi, None)],
        [sds((S, 3 * W), BF)], [pltpu.VMEM((W, S), F32), pltpu.VMEM((HG, S), F32)], 5 * dense)
    g_qkv = dot_tn(h_all, dqkv).astype(BF)
    three = blocks_of(g_qkv)

    part = dot_nt(after(dqkv, g_qkv), w_g).astype(BF).reshape(Y, 2, F, D)
    part = part[:, 0].astype(F32) + mate(part[:, 1]).astype(F32)
    far = [shift(part[s].astype(BF), "y", Y, -s) for s in range(1, Y)]
    dh1 = sum((r.astype(F32) for r in far), part[0])
    _, norm_back_one = jax.vjp(layer_norm, flat_in, ln1_gain, ln1_bias)
    dx, g_ln1g, g_ln1b = norm_back_one(dh1)
    grad_inputs = (dy1 + dx).reshape(1, F, D)

    one = over_z(over_x(over_y(one)))[0, 0]
    two = over_y(over_z(over_x(two)))[0, 0]
    three = over_z(over_x(three))[0, 0]
    ra = w_down.shape[0] // B
    one = spread(one)
    g_w_down, g_w_out = one[:ra], one[ra:]
    g_w_up = spread(two)
    e = everywhere(three)
    g_w_qkv = jnp.concatenate([e[yy][cc][:, p * W : (p + 1) * W] for p in range(3) for yy in range(Y) for cc in range(2)],
                              axis=1).astype(F32)

    def total(v):
        return jnp.sum(v.astype(F32), axis=0)

    def place(v):
        return lax.dynamic_update_slice_in_dim(jnp.zeros((D,), F32), v, group * W, 0)

    cols = total(dqkv)
    vecs = [g_ln1g, g_ln1b, place(cols[:W]), place(cols[2 * W :]), total(da), g_ln2g, g_ln2b, total(du), total(up)]
    flat = jnp.concatenate([v.reshape(B, -1) for v in vecs], axis=1)
    flat = flat + mate(flat)
    flat = sum((shift(flat, "y", Y, s) for s in range(1, Y)), flat)

    def scatter32(parts, axis, n, me):
        sent = [shift(lax.dynamic_index_in_dim(parts, (me + s) % n, 0, keepdims=False), axis, n, s) for s in range(1, n)]
        return sum(sent, lax.dynamic_index_in_dim(parts, me, 0, keepdims=False))

    flat = scatter32(jnp.moveaxis(flat.reshape(Z, X, -1), 1, 0), "x", X, xi)
    flat = scatter32(flat, "z", Z, zi)
    out, at = [], 0
    for v in vecs:
        n = v.shape[0] // B
        out.append(flat[at : at + n])
        at += n
    g_ln1g, g_ln1b, g_bq, g_bv, g_bo, g_ln2g, g_ln2b, g_bu, g_bd = out
    return (result.reshape(1, F, D), grad_inputs, g_ln1g, g_ln1b, g_w_qkv, g_bq, g_bv, g_w_out, g_bo, g_ln2g, g_ln2b,
            g_w_up, g_bu, g_w_down, g_bd)


def solution(mesh):
    batch, blk = mesh.shape["batch"], mesh.shape["blk"]
    Y = blk // 2
    X = Y if batch % Y == 0 else 1
    Z = batch // X
    fine = Mesh(mesh.devices.reshape(Z, X, Y, 2), ("z", "x", "y", "c"))
    rows, slots = ("z", "x"), ("y", "c")
    act = P(rows, slots, None)
    flat, mat = P(rows), P(rows, None)
    return jax.shard_map(
        functools.partial(shards, Z, X, Y),
        mesh=fine,
        in_specs=(act,) + (P(),) * 13 + (P(rows, None, None), act),
        out_specs=(act, act, flat, flat, mat, flat, flat, mat, flat, flat, flat, mat, flat, mat, flat),
        check_vma=False,
    )
```

time: 1240 us -> 430 us (0.35)
  waiting for transfers between devices: 614 us -> 156 us
  matrix products: 297 us -> 72.8 us
  local copies, waits for them, and re-layouts: 132 us -> 13.7 us
  starting transfers between devices: 0.84 us -> 71.7 us
  other arithmetic: 133 us -> 71 us
  blocking collectives: 41 us -> 0 us
  Pallas kernels: 0 us -> 34.5 us
  between operations: 16 us -> 2.44 us
    reduce_scatter x6 -> x0, waiting for transfers between devices: 534 us -> none  [the longest x1 152 us: shards(): lax.psum_scatter(grad_w_down.astype(jnp.bfloat16), 'batch', scatter_dimen...]
    dot_general x68 -> x15, matrix products: 297 us -> 72.8 us  [the longest x7 30.3 us: dot_tn(): lax.dot_general(a, b, (((0,), (0,)), ((), ())), preferred_element_type=F32)]
    ppermute x0 -> x40, waiting for transfers between devices: none -> 156 us  [the longest x24 136 us: shift(): return lax.ppermute(v, axis, [(i, (i + s) % n) for i in range(n)])]
    ppermute x0 -> x40, starting transfers between devices: none -> 71.7 us  [the longest x24 65.6 us: shift(): return lax.ppermute(v, axis, [(i, (i + s) % n) for i in range(n)])]
    broadcast_in_dim x16 -> x2, other arithmetic: 64.6 us -> 0.51 us  [the longest x1 0.33 us: over_z(): return scatter(g, 'z', Z, zi)[None]]
    all_gather x2 -> x0, waiting for transfers between devices: 62.5 us -> none  [the longest x1 32.4 us: shards(): lax.all_gather(value_rows, 'blk', axis=1, tiled=True)]
    dynamic_slice x56 -> x5, local copies, waits for them, and re-layouts: 57 us -> 3.22 us  [the longest x1 1.49 us: cols_of(): lax.dynamic_slice_in_dim(w, part * D + g * W, W, w.ndim - 1)]
    unnamed x1 -> x0, blocking collectives: 35.3 us -> none
  transfers between devices with their start and end apart: 9 -> 40, of which waited for: 9 -> 17; matrix products, arithmetic and copies ran while one was open for 6% -> 21% of each run, Pallas kernels for 0% -> 5%
where the time goes in v1:
time: 430 us; the launch traced here: 422 us
  waiting for transfers between devices  156 us (36%)
  matrix products  72.8 us (17%)
  starting transfers between devices  71.7 us (17%)
  other arithmetic  71 us (17%)
  Pallas kernels  34.5 us (8%)
  local copies, waits for them, and re-layouts  13.7 us (3%)
    ppermute x24, waiting for transfers between devices, shift(): return lax.ppermute(v, axis, [(i, (i + s) % n) for i in range(n)])  136 us
    ppermute x24, starting transfers between devices, shift(): return lax.ppermute(v, axis, [(i, (i + s) % n) for i in range(n)])  65.6 us
    pallas_call x2, Pallas kernels, attend(): pl.pallas_call(kernel, out_shape=outs, grid_spec=pltpu.PrefetchScalarGrid...  34.5 us
    dot_general x7, matrix products, dot_tn(): lax.dot_general(a, b, (((0,), (0,)), ((), ())), preferred_element_type=F32)  30.3 us
    dot_general x4, matrix products, dot_nt(): lax.dot_general(a, b, (((1,), (1,)), ((), ())), preferred_element_type=F32)  23.8 us
    convert_element_type x1, other arithmetic, shards(): du = gelu_back(dg.astype(F32))[0].astype(BF)  22.3 us
    ppermute x6, waiting for transfers between devices, hop(): return lax.ppermute(v, ('y', 'c'), pairs)  18.8 us
    dot_general x4, matrix products, dot(): return jnp.dot(a, b, preferred_element_type=F32)  18.8 us
  transfers between devices with their start and end apart: 40, of which 17 were waited for; matrix products, arithmetic and copies ran while one was open for 21% of the time, Pallas kernels for 5%

profile of v1, /device:TPU:0, one launch (start us, length us, event | category | flops | bytes accessed | tf_op | source)
XLA Modules:
  0.0 421.9 jit_solution(9524819312875640725)
XLA Ops:
  0.7 1.6 convert_reduce_fusion.3
  2.3 1.6 fusion.35
  3.9 2.7 fusion.33
  6.7 3.0 collective-permute-start.1
  13.2 1.5 constant_dynamic-slice_fusion.21
  14.8 18.3 %collective-permute-done.1 = bf16[512,1024]{1,0:T(8,128)(2,1)} collective-permute-done((bf16[512,1024]{1,0:T(8,128)(2,1)}, bf16[512,1024]{1,0:T(8,128)(2,1)}, u32[]{:S(2)}, u32[]{:S(2)}) %collective-permute-start.1) | collective-permute-done | bytes 1048608 | tf_op jit(solution)/shard_map/ppermute | solution.py:182
  33.1 9.6 %convolution_convert_fusion = bf16[512,4096]{1,0:T(8,128)(2,1)} fusion(bf16[512,1024]{1,0:T(8,128)(2,1)S(1)} %bitcast.224, bf16[4096,1024]{1,0:T(8,128)(2,1)} %param.28), kind=kOutput, calls=%fused_computation.30 | convolution fusion | flops 4297064448 | bytes 13631488 | tf_op jit(solution)/shard_map/dot_general | solution.py:35
  42.7 2.1 pad_maximum_fusion
  44.8 3.6 fusion.15.q_ref.k_ref.v_ref
  48.5 13.2 %shard_map.271 = (bf16[2048,256]{1,0:T(8,128)(2,1)S(1)}, f32[4,2048]{1,0:T(4,128)S(1)}) custom-call(s32[8,8]{1,0:T(8,128)S(1)} %select_reduce_fusion.3.lst, s32[8]{0:T(128)S(1)} %get-tuple-element.65.cnt, s32[8]{0:T(128)S(1)} %bitcast.219, bf16[2048,768]{1,0:T(8,128)(2,1)S(1)} %fusion.15.q_ref.k_ref.v_ref, bf16[2048,768]{1,0:T(8,128)(2,1)S(1)} %fusion.15.q_ref.k_ref.v_ref, ...), custom_call_target="tpu_custom_call" | custom-call | flops 1073741824 | bytes 10534912 | tf_op jit(solution)/shard_map/pallas_call | solution.py:139
  63.1 1.7 collective-permute-start.4
  64.9 7.7 %collective-permute-done.4 = bf16[512,256]{1,0:T(8,128)(2,1)} collective-permute-done((bf16[512,256]{1,0:T(8,128)(2,1)}, bf16[512,256]{1,0:T(8,128)(2,1)}, u32[]{:S(2)}, u32[]{:S(2)}) %collective-permute-start.4) | collective-permute-done | bytes 262176 | tf_op jit(solution)/shard_map/ppermute | solution.py:191
  72.6 3.9 collective-permute-done.5
  76.5 1.3 pad_maximum_fusion.7
  79.1 1.4 fusion.94
  81.3 1.3 slice-done.1
  82.7 4.5 %fusion.95 = f32[512,4096]{1,0:T(8,128)S(1)} fusion(bf16[512,1024]{1,0:T(8,128)(2,1)S(1)} %add_convert_fusion.5, bf16[1024,4096]{1,0:T(8,128)(2,1)S(1)} %bitcast.252), kind=kOutput, calls=%fused_computation.280 | convolution fusion | flops 4294967296 | bytes 17825792 | tf_op jit(solution)/shard_map/dot_general | solution.py:27
  87.2 22.3 %fusion.5 = (bf16[512,4096]{1,0:T(8,128)(2,1)}, f32[512,4096]{1,0:T(8,128)}) fusion(bf16[512,4096]{1,0:T(8,128)(2,1)S(1)} %copy-done.21, f32[512,4096]{1,0:T(8,128)S(1)} %fusion.95, f32[4096]{0:T(1024)S(1)} %copy-done.37), kind=kLoop, calls=%fused_computation.8 | loop fusion | flops 155189248 | bytes 25182208 | tf_op jit(solution)/shard_map/convert_element_type | solution.py:253
  109.5 9.8 %multiply_convert_fusion = bf16[512,4096]{1,0:T(8,128)(2,1)} fusion(f32[512,4096]{1,0:T(8,128)} %get-tuple-element.64, f32[512,4096]{1,0:T(8,128)} %copy-done.4, f32[4096]{0:T(1024)S(1)} %copy-done.37), kind=kLoop, calls=%fused_computation.14 | loop fusion | flops 8388608 | bytes 20987904 | tf_op jit(solution)/shard_map/convert_element_type | solution.py:252
  119.3 6.7 %convolution_convert_fusion.1 = bf16[4096,512]{1,0:T(8,128)(2,1)} fusion(bf16[512,4096]{1,0:T(8,128)(2,1)} %multiply_convert_fusion, bf16[1,512,1024]{2,1,0:T(8,128)(2,1)S(1)} %copy-done.17, s32[]{:T(128)S(6)} %select_n.330), kind=kOutput, calls=%fused_computation.31 | convolution fusion | flops 2149580800 | bytes 8912900 | tf_op jit(solution)/shard_map/dot_general | solution.py:31
  126.6 8.1 %multiply_reduce_fusion = (f32[1024]{0:T(1024)S(1)}, f32[512]{0:T(512)S(1)}, f32[1024]{0:T(1024)S(1)}, f32[512,1024]{1,0:T(8,128)S(1)}) fusion(f32[512,1024]{1,0:T(8,128)S(1)} %get-tuple-element.127, f32[512]{0:T(512)S(1)} %fusion.85, f32[512]{0:T(512)S(1)} %broadcast_multiply_fusion, f32[1024]{0:T(1024)S(1)} %copy-done.39, ...), kind=kOutput, calls=%fused_computation.82 | convolution fusion | flops 4299159040 | bytes 16795648 | tf_op jit(solution)/shard_map/dot_general | solution.py:35
  135.4 1.3 copy-done.7
  137.2 2.3 convolution_convert_fusion.5
  139.5 4.4 %convolution_convert_fusion.2 = bf16[1024,2048]{1,0:T(8,128)(2,1)} fusion(bf16[512,1024]{1,0:T(8,128)(2,1)S(1)} %copy-done.24, bf16[512,4096]{1,0:T(8,128)(2,1)S(1)} %copy-done.10, s32[]{:T(128)S(6)} %select_n.338), kind=kOutput, calls=%fused_computation.44 | convolution fusion | flops 2149580800 | bytes 7340036 | tf_op jit(solution)/shard_map/dot_general | solution.py:31
  144.2 3.3 convolution_convert_fusion.6
  148.2 1.8 collective-permute-start.7
  150.0 9.2 %add_convert_fusion.4 = bf16[512,1024]{1,0:T(8,128)(2,1)} fusion(f32[512,1024]{1,0:T(8,128)} %copy-done.9, bf16[512,4096]{1,0:T(8,128)(2,1)S(1)} %copy-done.19, bf16[4096,1024]{1,0:T(8,128)(2,1)} %param.28, f32[1024]{0:T(1024)S(1)} %copy-done.42), kind=kOutput, calls=%fused_computation.89 | convolution fusion | flops 4296540160 | bytes 15732736 | tf_op jit(solution)/shard_map/dot_general | solution.py:27
  160.4 7.1 %collective-permute-done.8 = bf16[512,256]{1,0:T(8,128)(2,1)S(1)} collective-permute-done((bf16[512,256]{1,0:T(8,128)(2,1)S(1)}, bf16[512,256]{1,0:T(8,128)(2,1)S(1)}, u32[]{:S(2)}, u32[]{:S(2)}) %collective-permute-start.8) | collective-permute-done | bytes 262176 | tf_op jit(solution)/shard_map/ppermute | solution.py:191
  168.2 1.2 pad_maximum_fusion.9.do_ref
  169.4 2.9 add_convert_fusion.3
  172.4 4.7 %add_convert_fusion = bf16[4096,512]{1,0:T(8,128)(2,1)S(1)} fusion(bf16[4096,512]{1,0:T(8,128)(2,1)} %collective-permute-done.25, bf16[512,4096]{1,0:T(8,128)(2,1)S(1)} %copy-done.20, bf16[512,1024]{1,0:T(8,128)(2,1)S(1)} %bitcast.225, s32[]{:T(128)S(6)} %select_n.339), kind=kOutput, calls=%fused_computation.11 | convolution fusion | flops 2153775104 | bytes 13107204 | tf_op jit(solution)/shard_map/dot_general | solution.py:31
  177.7 2.5 fusion.25
  181.1 4.6 %add_convert_fusion.1 = bf16[1024,2048]{1,0:T(8,128)(2,1)S(1)} fusion(bf16[1024,2048]{1,0:T(8,128)(2,1)} %collective-permute-done.9, bf16[512,1024]{1,0:T(8,128)(2,1)S(1)} %copy-done.25, bf16[512,4096]{1,0:T(8,128)(2,1)S(1)} %copy-done.12, s32[]{:T(128)S(6)} %select_n.337), kind=kOutput, calls=%fused_computation.13 | convolution fusion | flops 2153775104 | bytes 11534340 | tf_op jit(solution)/shard_map/dot_general | solution.py:31
  185.8 21.3 %shard_map.272 = bf16[2048,768]{1,0:T(8,128)(2,1)S(1)} custom-call(s32[8,8]{1,0:T(8,128)S(1)} %select_reduce_fusion.2.lst, s32[8]{0:T(128)S(1)} %get-tuple-element.122.cnt, s32[8]{0:T(128)S(1)} %bitcast.220, bf16[2048,768]{1,0:T(8,128)(2,1)S(1)} %copy-done.3, bf16[2048,768]{1,0:T(8,128)(2,1)S(1)} %copy-done.3, bf16[2048,768]{1,0:T(8,128)(2,1)S(1)} %copy-done.3, ...), custom_call_target="tpu_custom_call" | custom-call | flops 2684354560 | bytes 14729216 | tf_op jit(solution)/shard_map/pallas_call | solution.py:139
  207.1 3.7 convolution_convert_fusion.4
  210.8 9.9 %collective-permute-start.19 = (bf16[4,128,768]{2,1,0:T(8,128)(2,1)S(1)}, bf16[4,128,768]{2,1,0:T(8,128)(2,1)S(1)}, u32[]{:S(2)}, u32[]{:S(2)}) collective-permute-start(bf16[4,128,768]{2,1,0:T(8,128)(2,1)S(1)} %dynamic-slice_bitcast_fusion.2), channel_id=1, source_target_pairs={{0,4},{4,0},{1,5},{5,1},{2,6},{6,2},{3,7},{7,3},{8,12},{12,8},{9,1... | collective-permute-start | bytes 2359304 | tf_op jit(solution)/shard_map/ppermute | solution.py:182
  221.0 3.9 convolution_convert_fusion.3
  224.9 14.2 %collective-permute-done.19 = bf16[4,128,768]{2,1,0:T(8,128)(2,1)S(1)} collective-permute-done((bf16[4,128,768]{2,1,0:T(8,128)(2,1)S(1)}, bf16[4,128,768]{2,1,0:T(8,128)(2,1)S(1)}, u32[]{:S(2)}, u32[]{:S(2)}) %collective-permute-start.19) | collective-permute-done | bytes 786464 | tf_op jit(solution)/shard_map/ppermute | solution.py:182
  239.5 4.0 collective-permute-start.22
  243.6 5.5 %collective-permute-done.20 = bf16[1,128,768]{2,1,0:T(8,128)(2,1)S(1)} collective-permute-done((bf16[1,128,768]{2,1,0:T(8,128)(2,1)S(1)}, bf16[1,128,768]{2,1,0:T(8,128)(2,1)S(1)}, u32[]{:S(2)}, u32[]{:S(2)}) %collective-permute-start.20) | collective-permute-done | bytes 196640 | tf_op jit(solution)/shard_map/ppermute | solution.py:182
  249.1 6.5 %collective-permute-done.21 = bf16[1,128,768]{2,1,0:T(8,128)(2,1)S(1)} collective-permute-done((bf16[1,128,768]{2,1,0:T(8,128)(2,1)S(1)}, bf16[1,128,768]{2,1,0:T(8,128)(2,1)S(1)}, u32[]{:S(2)}, u32[]{:S(2)}) %collective-permute-start.21) | collective-permute-done | bytes 196640 | tf_op jit(solution)/shard_map/ppermute | solution.py:182
  258.5 10.1 %collective-permute-done.24 = bf16[2,128,768]{2,1,0:T(8,128)(2,1)S(1)} collective-permute-done((bf16[2,128,768]{2,1,0:T(8,128)(2,1)S(1)}, bf16[2,128,768]{2,1,0:T(8,128)(2,1)S(1)}, u32[]{:S(2)}, u32[]{:S(2)}) %collective-permute-start.24) | collective-permute-done | bytes 393248 | tf_op jit(solution)/shard_map/ppermute | solution.py:182
  268.9 1.3 convert_element_type.293
  270.2 13.3 %collective-permute-done.33 = bf16[4,128,2048]{2,1,0:T(8,128)(2,1)S(1)} collective-permute-done((bf16[4,128,2048]{2,1,0:T(8,128)(2,1)S(1)}, bf16[4,128,2048]{2,1,0:T(8,128)(2,1)S(1)}, u32[]{:S(2)}, u32[]{:S(2)}) %collective-permute-start.33) | collective-permute-done | bytes 2097184 | tf_op jit(solution)/shard_map/ppermute | solution.py:182
  284.6 3.7 collective-permute-start.36
  290.4 10.8 %collective-permute-done.34 = bf16[1,128,2048]{2,1,0:T(8,128)(2,1)S(1)} collective-permute-done((bf16[1,128,2048]{2,1,0:T(8,128)(2,1)S(1)}, bf16[1,128,2048]{2,1,0:T(8,128)(2,1)S(1)}, u32[]{:S(2)}, u32[]{:S(2)}) %collective-permute-start.34) | collective-permute-done | bytes 524320 | tf_op jit(solution)/shard_map/ppermute | solution.py:182
  301.2 21.0 %collective-permute-done.35 = bf16[1,128,2048]{2,1,0:T(8,128)(2,1)S(1)} collective-permute-done((bf16[1,128,2048]{2,1,0:T(8,128)(2,1)S(1)}, bf16[1,128,2048]{2,1,0:T(8,128)(2,1)S(1)}, u32[]{:S(2)}, u32[]{:S(2)}) %collective-permute-start.35) | collective-permute-done | bytes 524320 | tf_op jit(solution)/shard_map/ppermute | solution.py:182
  323.8 3.1 fusion.13
  327.0 1.1 dynamic-slice_bitcast_fusion.1
  328.1 1.4 collective-permute-start.27
  333.1 1.8 add_bitcast_fusion
  334.9 1.2 collective-permute-start.14
  339.2 1.2 collective-permute-start.15
  340.3 16.8 %collective-permute-done.27 = bf16[4,640,256]{2,1,0:T(8,128)(2,1)S(1)} collective-permute-done((bf16[4,640,256]{2,1,0:T(8,128)(2,1)}, bf16[4,640,256]{2,1,0:T(8,128)(2,1)S(1)}, u32[]{:S(2)}, u32[]{:S(2)}) %collective-permute-start.27) | collective-permute-done | bytes 1310752 | tf_op jit(solution)/shard_map/ppermute | solution.py:182
  357.1 1.6 fusion.29
  358.9 11.8 %collective-permute-start.28 = (bf16[1,640,256]{2,1,0:T(8,128)(2,1)S(1)}, bf16[1,640,256]{2,1,0:T(8,128)(2,1)S(1)}, u32[]{:S(2)}, u32[]{:S(2)}) collective-permute-start(bf16[1,640,256]{2,1,0:T(8,128)(2,1)S(1)} %get-tuple-element.79), channel_id=1, source_target_pairs={{0,8},{8,16},{16,24},{24,0},{1,9},{9,17},{17,25},{25,1},{2,10},{10... | collective-permute-start | bytes 983048 | tf_op jit(solution)/shard_map/ppermute | solution.py:182
  370.7 2.4 collective-permute-start.30
  373.3 5.6 %collective-permute-done.28 = bf16[1,640,256]{2,1,0:T(8,128)(2,1)S(1)} collective-permute-done((bf16[1,640,256]{2,1,0:T(8,128)(2,1)S(1)}, bf16[1,640,256]{2,1,0:T(8,128)(2,1)S(1)}, u32[]{:S(2)}, u32[]{:S(2)}) %collective-permute-start.28) | collective-permute-done | bytes 327712 | tf_op jit(solution)/shard_map/ppermute | solution.py:182
  378.9 16.1 %collective-permute-start.17 = (f32[1536]{0:T(1024)S(1)}, f32[1536]{0:T(1024)S(1)}, u32[]{:S(2)}, u32[]{:S(2)}) collective-permute-start(f32[1536]{0:T(1024)S(1)} %get-tuple-element.49), channel_id=1, source_target_pairs={{0,16},{8,24},{16,0},{24,8},{1,17},{9,25},{17,1},{25,9},{2,18},{10... | collective-permute-start | bytes 18440 | tf_op jit(solution)/shard_map/ppermute | solution.py:182
  394.9 5.0 %collective-permute-start.18 = (f32[1536]{0:T(1024)S(1)}, f32[1536]{0:T(1024)S(1)}, u32[]{:S(2)}, u32[]{:S(2)}) collective-permute-start(f32[1536]{0:T(1024)S(1)} %get-tuple-element.48), channel_id=1, source_target_pairs={{0,24},{8,0},{16,8},{24,16},{1,25},{9,1},{17,9},{25,17},{2,26},{10... | collective-permute-start | bytes 18440 | tf_op jit(solution)/shard_map/ppermute | solution.py:182
  402.5 1.2 collective-permute-start.32
  404.9 1.5 maximum_convert_fusion
  406.5 12.3 %collective-permute-done.32 = bf16[2,640,256]{2,1,0:T(8,128)(2,1)S(1)} collective-permute-done((bf16[2,640,256]{2,1,0:T(8,128)(2,1)S(1)}, bf16[2,640,256]{2,1,0:T(8,128)(2,1)S(1)}, u32[]{:S(2)}, u32[]{:S(2)}) %collective-permute-start.32) | collective-permute-done | bytes 655392 | tf_op jit(solution)/shard_map/ppermute | solution.py:182
  419.0 1.6 fusion.46
  (264 shorter events, 33.2 us)
Async XLA Ops:
  0.6 78.4 %copy-start = (bf16[1024,1024]{1,0:T(8,128)(2,1)S(1)}, bf16[1024,1024]{1,0:T(8,128)(2,1)}, u32[]{:S(2)}) copy-start(bf16[1024,1024]{1,0:T(8,128)(2,1)} %param.22) | copy-start | bytes 6291460
  0.7 9.1 %copy-start.43 = (s32[1,2,3]{2,1,0:T(2,128)S(1)}, s32[1,2,3]{2,1,0:T(2,128)}, u32[]{:S(2)}) copy-start(s32[1,2,3]{2,1,0:T(2,128)} %param.30) | copy-start | bytes 76
  3.9 29.2 %copy-start.16 = (bf16[1,512,1024]{2,1,0:T(8,128)(2,1)S(1)}, bf16[1,512,1024]{2,1,0:T(8,128)(2,1)}, u32[]{:S(2)}) copy-start(bf16[1,512,1024]{2,1,0:T(8,128)(2,1)} %param.31) | copy-start | bytes 3145732
  6.7 26.4 %collective-permute-start.1 = (bf16[512,1024]{1,0:T(8,128)(2,1)}, bf16[512,1024]{1,0:T(8,128)(2,1)}, u32[]{:S(2)}, u32[]{:S(2)}) collective-permute-start(bf16[512,1024]{1,0:T(8,128)(2,1)} %fusion.33), channel_id=1, source_target_pairs={{0,2},{2,0},{1,3},{3,1},{4,6},{6,4},{5,7},{7,5},{8,10},{10,8},{9,1... | collective-permute-start | bytes 3145736 | tf_op jit(solution)/shard_map/ppermute | solution.py:182
  9.6 33.0 %collective-permute-start = (bf16[512,1024]{1,0:T(8,128)(2,1)}, bf16[512,1024]{1,0:T(8,128)(2,1)}, u32[]{:S(2)}, u32[]{:S(2)}) collective-permute-start(bf16[512,1024]{1,0:T(8,128)(2,1)} %fusion.33), channel_id=1, source_target_pairs={{0,1},{1,0},{2,3},{3,2},{4,5},{5,4},{6,7},{7,6},{8,9},{9,8},{10,11... | collective-permute-start | bytes 3145736 | tf_op jit(solution)/shard_map/ppermute | solution.py:185
  14.7 30.1 %copy-start.29 = (bf16[1024,256]{1,0:T(8,128)(2,1)}, bf16[1024,256]{1,0:T(8,128)(2,1)S(1)}, u32[]{:S(2)}) copy-start(bf16[1024,256]{1,0:T(8,128)(2,1)S(1)} %get-tuple-element.67) | copy-start | bytes 1572868
  14.7 30.1 %copy-start.31 = (bf16[1024,256]{1,0:T(8,128)(2,1)}, bf16[1024,256]{1,0:T(8,128)(2,1)S(1)}, u32[]{:S(2)}) copy-start(bf16[1024,256]{1,0:T(8,128)(2,1)S(1)} %get-tuple-element.68) | copy-start | bytes 1572868
  14.8 30.1 %copy-start.33 = (bf16[1024,256]{1,0:T(8,128)(2,1)}, bf16[1024,256]{1,0:T(8,128)(2,1)S(1)}, u32[]{:S(2)}) copy-start(bf16[1024,256]{1,0:T(8,128)(2,1)S(1)} %get-tuple-element.69) | copy-start | bytes 1572868
  33.1 9.6 %collective-permute-start.2 = (bf16[512,1024]{1,0:T(8,128)(2,1)}, bf16[512,1024]{1,0:T(8,128)(2,1)S(1)}, u32[]{:S(2)}, u32[]{:S(2)}) collective-permute-start(bf16[512,1024]{1,0:T(8,128)(2,1)} %collective-permute-done.1), channel_id=1, source_target_pairs={{0,1},{1,0},{2,3},{3,2},{4,5},{5,4},{6,7},{7,6},{8,9},{9,8},{10,11... | collective-permute-start | bytes 3145736 | tf_op jit(solution)/shard_map/ppermute | solution.py:185
  48.5 13.2 %copy-start.2 = (bf16[2048,768]{1,0:T(8,128)(2,1)}, bf16[2048,768]{1,0:T(8,128)(2,1)S(1)}, u32[]{:S(2)}) copy-start(bf16[2048,768]{1,0:T(8,128)(2,1)S(1)} %fusion.15.q_ref.k_ref.v_ref) | copy-start | bytes 9437188
  62.6 2.2 collective-permute-start.3
  63.1 9.5 %collective-permute-start.4 = (bf16[512,256]{1,0:T(8,128)(2,1)}, bf16[512,256]{1,0:T(8,128)(2,1)}, u32[]{:S(2)}, u32[]{:S(2)}) collective-permute-start(bf16[512,256]{1,0:T(8,128)(2,1)} %get-tuple-element.97), channel_id=1, source_target_pairs={{0,2},{1,3},{2,0},{3,1},{4,6},{5,7},{6,4},{7,5},{8,10},{9,11},{10,... | collective-permute-start | bytes 786440 | tf_op jit(solution)/shard_map/ppermute | solution.py:191
  64.9 11.7 %collective-permute-start.5 = (bf16[512,256]{1,0:T(8,128)(2,1)}, bf16[512,256]{1,0:T(8,128)(2,1)}, u32[]{:S(2)}, u32[]{:S(2)}) collective-permute-start(bf16[512,256]{1,0:T(8,128)(2,1)} %get-tuple-element.96), channel_id=1, source_target_pairs={{0,3},{1,2},{2,1},{3,0},{4,7},{5,6},{6,5},{7,4},{8,11},{9,10},{10,... | collective-permute-start | bytes 786440 | tf_op jit(solution)/shard_map/ppermute | solution.py:191
  80.5 54.2 %copy-start.9 = (f32[512,1024]{1,0:T(8,128)}, f32[512,1024]{1,0:T(8,128)S(1)}, u32[]{:S(2)}) copy-start(f32[512,1024]{1,0:T(8,128)S(1)} %get-tuple-element.127) | copy-start | bytes 6291460
  82.7 4.5 %copy-start.23 = (bf16[512,1024]{1,0:T(8,128)(2,1)}, bf16[512,1024]{1,0:T(8,128)(2,1)S(1)}, u32[]{:S(2)}) copy-start(bf16[512,1024]{1,0:T(8,128)(2,1)S(1)} %add_convert_fusion.5) | copy-start | bytes 3145732
  82.7 4.5 %copy-start.21 = (bf16[512,4096]{1,0:T(8,128)(2,1)S(1)}, bf16[512,4096]{1,0:T(8,128)(2,1)}, u32[]{:S(2)}) copy-start(bf16[512,4096]{1,0:T(8,128)(2,1)} %convolution_convert_fusion) | copy-start | bytes 12582916
  82.7 4.5 %copy-start.37 = (f32[4096]{0:T(1024)S(1)}, f32[4096]{0:T(1024)}, u32[]{:S(2)}) copy-start(f32[4096]{0:T(1024)} %param.27) | copy-start | bytes 49156
  87.2 22.3 %copy-start.4 = (f32[512,4096]{1,0:T(8,128)}, f32[512,4096]{1,0:T(8,128)S(1)}, u32[]{:S(2)}) copy-start(f32[512,4096]{1,0:T(8,128)S(1)} %fusion.95) | copy-start | bytes 25165828
  109.5 9.9 %copy-start.17 = (bf16[1,512,1024]{2,1,0:T(8,128)(2,1)S(1)}, bf16[1,512,1024]{2,1,0:T(8,128)(2,1)}, u32[]{:S(2)}) copy-start(bf16[1,512,1024]{2,1,0:T(8,128)(2,1)} %param.31) | copy-start | bytes 3145732
  119.3 7.3 %copy-start.10 = (bf16[512,4096]{1,0:T(8,128)(2,1)S(1)}, bf16[512,4096]{1,0:T(8,128)(2,1)}, u32[]{:S(2)}) copy-start(bf16[512,4096]{1,0:T(8,128)(2,1)} %get-tuple-element.35) | copy-start | bytes 12582916
  126.0 46.3 %collective-permute-start.25 = (bf16[4096,512]{1,0:T(8,128)(2,1)}, bf16[4096,512]{1,0:T(8,128)(2,1)}, u32[]{:S(2)}, u32[]{:S(2)}) collective-permute-start(bf16[4096,512]{1,0:T(8,128)(2,1)} %convolution_convert_fusion.1), channel_id=1, source_target_pairs={{0,1},{1,0},{2,3},{3,2},{4,5},{5,4},{6,7},{7,6},{8,9},{9,8},{10,11... | collective-permute-start | bytes 12582920 | tf_op jit(solution)/shard_map/ppermute | solution.py:185
  143.9 6.1 %copy-start.42 = (f32[1024]{0:T(1024)S(1)}, f32[1024]{0:T(1024)}, u32[]{:S(2)}) copy-start(f32[1024]{0:T(1024)} %param.29) | copy-start | bytes 12292
  143.9 36.8 %collective-permute-start.9 = (bf16[1024,2048]{1,0:T(8,128)(2,1)}, bf16[1024,2048]{1,0:T(8,128)(2,1)}, u32[]{:S(2)}, u32[]{:S(2)}) collective-permute-start(bf16[1024,2048]{1,0:T(8,128)(2,1)} %convolution_convert_fusion.2), channel_id=1, source_target_pairs={{0,1},{1,0},{2,3},{3,2},{4,5},{5,4},{6,7},{7,6},{8,9},{9,8},{10,11... | collective-permute-start | bytes 12582920 | tf_op jit(solution)/shard_map/ppermute | solution.py:185
  144.2 5.8 %copy-start.19 = (bf16[512,4096]{1,0:T(8,128)(2,1)S(1)}, bf16[512,4096]{1,0:T(8,128)(2,1)}, u32[]{:S(2)}) copy-start(bf16[512,4096]{1,0:T(8,128)(2,1)} %multiply_convert_fusion) | copy-start | bytes 12582916
  147.4 22.0 %collective-permute-start.10 = (bf16[1024,512]{1,0:T(8,128)(2,1)}, bf16[1024,512]{1,0:T(8,128)(2,1)}, u32[]{:S(2)}, u32[]{:S(2)}) collective-permute-start(bf16[1024,512]{1,0:T(8,128)(2,1)} %convolution_convert_fusion.6), channel_id=1, source_target_pairs={{0,1},{1,0},{2,3},{3,2},{4,5},{5,4},{6,7},{7,6},{8,9},{9,8},{10,11... | collective-permute-start | bytes 3145736 | tf_op jit(solution)/shard_map/ppermute | solution.py:185
  148.1 11.1 %collective-permute-start.6 = (bf16[512,256]{1,0:T(8,128)(2,1)S(1)}, bf16[512,256]{1,0:T(8,128)(2,1)S(1)}, u32[]{:S(2)}, u32[]{:S(2)}) collective-permute-start(bf16[512,256]{1,0:T(8,128)(2,1)S(1)} %get-tuple-element.90), channel_id=1, source_target_pairs={{0,1},{1,0},{2,3},{3,2},{4,5},{5,4},{6,7},{7,6},{8,9},{9,8},{10,11... | collective-permute-start | bytes 786440 | tf_op jit(solution)/shard_map/ppermute | solution.py:191
  148.2 11.2 %copy-start.11 = (bf16[512,4096]{1,0:T(8,128)(2,1)S(1)}, bf16[512,4096]{1,0:T(8,128)(2,1)}, u32[]{:S(2)}) copy-start(bf16[512,4096]{1,0:T(8,128)(2,1)} %get-tuple-element.35) | copy-start | bytes 12582916
  148.2 12.2 %collective-permute-start.7 = (bf16[512,256]{1,0:T(8,128)(2,1)S(1)}, bf16[512,256]{1,0:T(8,128)(2,1)S(1)}, u32[]{:S(2)}, u32[]{:S(2)}) collective-permute-start(bf16[512,256]{1,0:T(8,128)(2,1)S(1)} %get-tuple-element.89), channel_id=1, source_target_pairs={{0,2},{1,3},{2,0},{3,1},{4,6},{5,7},{6,4},{7,5},{8,10},{9,11},{10,... | collective-permute-start | bytes 786440 | tf_op jit(solution)/shard_map/ppermute | solution.py:191
  159.2 8.3 %collective-permute-start.8 = (bf16[512,256]{1,0:T(8,128)(2,1)S(1)}, bf16[512,256]{1,0:T(8,128)(2,1)S(1)}, u32[]{:S(2)}, u32[]{:S(2)}) collective-permute-start(bf16[512,256]{1,0:T(8,128)(2,1)S(1)} %get-tuple-element.88), channel_id=1, source_target_pairs={{0,3},{1,2},{2,1},{3,0},{4,7},{5,6},{6,5},{7,4},{8,11},{9,10},{10,... | collective-permute-start | bytes 786440 | tf_op jit(solution)/shard_map/ppermute | solution.py:191
  160.3 7.1 %copy-start.35 = (bf16[512,256]{1,0:T(8,128)(2,1)}, bf16[512,256]{1,0:T(8,128)(2,1)S(1)}, u32[]{:S(2)}) copy-start(bf16[512,256]{1,0:T(8,128)(2,1)S(1)} %collective-permute-done.7) | copy-start | bytes 786436
  180.2 5.5 %copy-start.3 = (bf16[2048,768]{1,0:T(8,128)(2,1)S(1)}, bf16[2048,768]{1,0:T(8,128)(2,1)}, u32[]{:S(2)}) copy-start(bf16[2048,768]{1,0:T(8,128)(2,1)} %copy-done.2) | copy-start | bytes 9437188
  180.2 143.5 %collective-permute-start.26 = (bf16[4,2,640,256]{3,2,1,0:T(8,128)(2,1)}, bf16[4,2,640,256]{3,2,1,0:T(8,128)(2,1)}, u32[]{:S(2)}, u32[]{:S(2)}) collective-permute-start(bf16[4,2,640,256]{3,2,1,0:T(8,128)(2,1)} %fusion.25), channel_id=1, source_target_pairs={{0,2},{2,0},{1,3},{3,1},{4,6},{6,4},{5,7},{7,5},{8,10},{10,8},{9,1... | collective-permute-start | bytes 7864328 | tf_op jit(solution)/shard_map/ppermute | solution.py:182
  185.8 21.3 %copy-start.15 = (bf16[2048,1024]{1,0:T(8,128)(2,1)S(1)}, bf16[2048,1024]{1,0:T(8,128)(2,1)}, u32[]{:S(2)}) copy-start(bf16[2048,1024]{1,0:T(8,128)(2,1)} %copy-done.14) | copy-start | bytes 12582916
  210.7 10.2 %copy-start.30 = (bf16[1024,256]{1,0:T(8,128)(2,1)S(1)}, bf16[1024,256]{1,0:T(8,128)(2,1)}, u32[]{:S(2)}) copy-start(bf16[1024,256]{1,0:T(8,128)(2,1)} %copy-done.29) | copy-start | bytes 1572868
  210.8 10.2 %copy-start.32 = (bf16[1024,256]{1,0:T(8,128)(2,1)S(1)}, bf16[1024,256]{1,0:T(8,128)(2,1)}, u32[]{:S(2)}) copy-start(bf16[1024,256]{1,0:T(8,128)(2,1)} %copy-done.31) | copy-start | bytes 1572868
  210.8 10.2 %copy-start.34 = (bf16[1024,256]{1,0:T(8,128)(2,1)S(1)}, bf16[1024,256]{1,0:T(8,128)(2,1)}, u32[]{:S(2)}) copy-start(bf16[1024,256]{1,0:T(8,128)(2,1)} %copy-done.33) | copy-start | bytes 1572868
  210.8 28.2 %collective-permute-start.19 = (bf16[4,128,768]{2,1,0:T(8,128)(2,1)S(1)}, bf16[4,128,768]{2,1,0:T(8,128)(2,1)S(1)}, u32[]{:S(2)}, u32[]{:S(2)}) collective-permute-start(bf16[4,128,768]{2,1,0:T(8,128)(2,1)S(1)} %dynamic-slice_bitcast_fusion.2), channel_id=1, source_target_pairs={{0,4},{4,0},{1,5},{5,1},{2,6},{6,2},{3,7},{7,3},{8,12},{12,8},{9,1... | collective-permute-start | bytes 2359304 | tf_op jit(solution)/shard_map/ppermute | solution.py:182
  220.9 62.5 %collective-permute-start.33 = (bf16[4,128,2048]{2,1,0:T(8,128)(2,1)S(1)}, bf16[4,128,2048]{2,1,0:T(8,128)(2,1)S(1)}, u32[]{:S(2)}, u32[]{:S(2)}) collective-permute-start(bf16[4,128,2048]{2,1,0:T(8,128)(2,1)S(1)} %dynamic-slice_bitcast_fusion), channel_id=1, source_target_pairs={{0,4},{4,0},{1,5},{5,1},{2,6},{6,2},{3,7},{7,3},{8,12},{12,8},{9,1... | collective-permute-start | bytes 6291464 | tf_op jit(solution)/shard_map/ppermute | solution.py:182
  239.4 9.8 %collective-permute-start.20 = (bf16[1,128,768]{2,1,0:T(8,128)(2,1)S(1)}, bf16[1,128,768]{2,1,0:T(8,128)(2,1)S(1)}, u32[]{:S(2)}, u32[]{:S(2)}) collective-permute-start(bf16[1,128,768]{2,1,0:T(8,128)(2,1)S(1)} %get-tuple-element.103), channel_id=1, source_target_pairs={{0,8},{8,16},{16,24},{24,0},{1,9},{9,17},{17,25},{25,1},{2,10},{10... | collective-permute-start | bytes 589832 | tf_op jit(solution)/shard_map/ppermute | solution.py:182
  239.4 16.2 %collective-permute-start.21 = (bf16[1,128,768]{2,1,0:T(8,128)(2,1)S(1)}, bf16[1,128,768]{2,1,0:T(8,128)(2,1)S(1)}, u32[]{:S(2)}, u32[]{:S(2)}) collective-permute-start(bf16[1,128,768]{2,1,0:T(8,128)(2,1)S(1)} %get-tuple-element.105), channel_id=1, source_target_pairs={{0,16},{8,24},{16,0},{24,8},{1,17},{9,25},{17,1},{25,9},{2,18},{10... | collective-permute-start | bytes 589832 | tf_op jit(solution)/shard_map/ppermute | solution.py:182
  239.5 16.1 %collective-permute-start.22 = (bf16[1,128,768]{2,1,0:T(8,128)(2,1)S(1)}, bf16[1,128,768]{2,1,0:T(8,128)(2,1)S(1)}, u32[]{:S(2)}, u32[]{:S(2)}) collective-permute-start(bf16[1,128,768]{2,1,0:T(8,128)(2,1)S(1)} %get-tuple-element.104), channel_id=1, source_target_pairs={{0,24},{8,0},{16,8},{24,16},{1,25},{9,1},{17,9},{25,17},{2,26},{10... | collective-permute-start | bytes 589832 | tf_op jit(solution)/shard_map/ppermute | solution.py:182
  249.1 39.2 %collective-permute-start.11 = (bf16[2,512,1024]{2,1,0:T(8,128)(2,1)S(1)}, bf16[2,512,1024]{2,1,0:T(8,128)(2,1)S(1)}, u32[]{:S(2)}, u32[]{:S(2)}) collective-permute-start(bf16[2,512,1024]{2,1,0:T(8,128)(2,1)S(1)} %slice_bitcast_fusion.1), channel_id=1, source_target_pairs={{0,1},{1,0},{2,3},{3,2},{4,5},{5,4},{6,7},{7,6},{8,9},{9,8},{10,11... | collective-permute-start | bytes 6291464 | tf_op jit(solution)/shard_map/ppermute | solution.py:185
  255.7 1.5 collective-permute-start.23
  257.3 11.2 %collective-permute-start.24 = (bf16[2,128,768]{2,1,0:T(8,128)(2,1)S(1)}, bf16[2,128,768]{2,1,0:T(8,128)(2,1)S(1)}, u32[]{:S(2)}, u32[]{:S(2)}) collective-permute-start(bf16[2,128,768]{2,1,0:T(8,128)(2,1)S(1)} %pad_maximum_fusion.16), channel_id=1, source_target_pairs={{0,2},{2,0},{1,3},{3,1},{4,6},{6,4},{5,7},{7,5},{8,10},{10,8},{9,1... | collective-permute-start | bytes 1179656 | tf_op jit(solution)/shard_map/ppermute | solution.py:182
  284.4 16.8 %collective-permute-start.34 = (bf16[1,128,2048]{2,1,0:T(8,128)(2,1)S(1)}, bf16[1,128,2048]{2,1,0:T(8,128)(2,1)S(1)}, u32[]{:S(2)}, u32[]{:S(2)}) collective-permute-start(bf16[1,128,2048]{2,1,0:T(8,128)(2,1)S(1)} %get-tuple-element.72), channel_id=1, source_target_pairs={{0,8},{8,16},{16,24},{24,0},{1,9},{9,17},{17,25},{25,1},{2,10},{10... | collective-permute-start | bytes 1572872 | tf_op jit(solution)/shard_map/ppermute | solution.py:182
  284.5 37.8 %collective-permute-start.35 = (bf16[1,128,2048]{2,1,0:T(8,128)(2,1)S(1)}, bf16[1,128,2048]{2,1,0:T(8,128)(2,1)S(1)}, u32[]{:S(2)}, u32[]{:S(2)}) collective-permute-start(bf16[1,128,2048]{2,1,0:T(8,128)(2,1)S(1)} %get-tuple-element.74), channel_id=1, source_target_pairs={{0,16},{8,24},{16,0},{24,8},{1,17},{9,25},{17,1},{25,9},{2,18},{10... | collective-permute-start | bytes 1572872 | tf_op jit(solution)/shard_map/ppermute | solution.py:182
  284.6 37.7 %collective-permute-start.36 = (bf16[1,128,2048]{2,1,0:T(8,128)(2,1)S(1)}, bf16[1,128,2048]{2,1,0:T(8,128)(2,1)S(1)}, u32[]{:S(2)}, u32[]{:S(2)}) collective-permute-start(bf16[1,128,2048]{2,1,0:T(8,128)(2,1)S(1)} %get-tuple-element.73), channel_id=1, source_target_pairs={{0,24},{8,0},{16,8},{24,16},{1,25},{9,1},{17,9},{25,17},{2,26},{10... | collective-permute-start | bytes 1572872 | tf_op jit(solution)/shard_map/ppermute | solution.py:182
  289.4 40.4 %collective-permute-start.12 = (bf16[512,1024]{1,0:T(8,128)(2,1)S(1)}, bf16[512,1024]{1,0:T(8,128)(2,1)S(1)}, u32[]{:S(2)}, u32[]{:S(2)}) collective-permute-start(bf16[512,1024]{1,0:T(8,128)(2,1)S(1)} %fusion.45), channel_id=1, source_target_pairs={{0,2},{2,0},{1,3},{3,1},{4,6},{6,4},{5,7},{7,5},{8,10},{10,8},{9,1... | collective-permute-start | bytes 3145736 | tf_op jit(solution)/shard_map/ppermute | solution.py:182
  322.8 6.8 %collective-permute-start.37 = (bf16[1,1,128,1024]{3,2,1,0:T(8,128)(2,1)S(1)}, bf16[1,1,128,1024]{3,2,1,0:T(8,128)(2,1)S(1)}, u32[]{:S(2)}, u32[]{:S(2)}) collective-permute-start(bf16[1,1,128,1024]{3,2,1,0:T(8,128)(2,1)S(1)} %fusion.61), channel_id=1, source_target_pairs={{0,2},{2,0},{1,3},{3,1},{4,6},{6,4},{5,7},{7,5},{8,10},{10,8},{9,1... | collective-permute-start | bytes 786440 | tf_op jit(solution)/shard_map/ppermute | solution.py:182
  328.1 29.0 %collective-permute-start.27 = (bf16[4,640,256]{2,1,0:T(8,128)(2,1)}, bf16[4,640,256]{2,1,0:T(8,128)(2,1)S(1)}, u32[]{:S(2)}, u32[]{:S(2)}) collective-permute-start(bf16[4,640,256]{2,1,0:T(8,128)(2,1)} %dynamic-slice_bitcast_fusion.1), channel_id=1, source_target_pairs={{0,4},{4,0},{1,5},{5,1},{2,6},{6,2},{3,7},{7,3},{8,12},{12,8},{9,1... | collective-permute-start | bytes 3932168 | tf_op jit(solution)/shard_map/ppermute | solution.py:182
  329.7 6.4 %collective-permute-start.38 = (bf16[128,1024]{1,0:T(8,128)(2,1)S(1)}, bf16[128,1024]{1,0:T(8,128)(2,1)S(1)}, u32[]{:S(2)}, u32[]{:S(2)}) collective-permute-start(bf16[128,1024]{1,0:T(8,128)(2,1)S(1)} %bitcast.229), channel_id=1, source_target_pairs={{0,1},{1,0},{2,3},{3,2},{4,5},{5,4},{6,7},{7,6},{8,9},{9,8},{10,11... | collective-permute-start | bytes 786440 | tf_op jit(solution)/shard_map/ppermute | solution.py:185
  330.9 4.0 collective-permute-start.13
  334.9 4.2 collective-permute-start.14
  337.6 66.1 %collective-permute-start.39 = (bf16[2,128,1024]{2,1,0:T(8,128)(2,1)}, bf16[2,128,1024]{2,1,0:T(8,128)(2,1)}, u32[]{:S(2)}, u32[]{:S(2)}) collective-permute-start(bf16[2,128,1024]{2,1,0:T(8,128)(2,1)} %pad_maximum_fusion.15), channel_id=1, source_target_pairs={{0,2},{2,0},{1,3},{3,1},{4,6},{6,4},{5,7},{7,5},{8,10},{10,8},{9,1... | collective-permute-start | bytes 1572872 | tf_op jit(solution)/shard_map/ppermute | solution.py:182
  339.2 34.0 %collective-permute-start.15 = (f32[4,1536]{1,0:T(4,128)S(1)}, f32[4,1536]{1,0:T(4,128)S(1)}, u32[]{:S(2)}, u32[]{:S(2)}) collective-permute-start(f32[4,1536]{1,0:T(4,128)S(1)} %bitcast.248), channel_id=1, source_target_pairs={{0,4},{4,0},{1,5},{5,1},{2,6},{6,2},{3,7},{7,3},{8,12},{12,8},{9,1... | collective-permute-start | bytes 73736 | tf_op jit(solution)/shard_map/ppermute | solution.py:182
  358.8 44.9 %copy-start.28 = (bf16[128,1024]{1,0:T(8,128)(2,1)S(1)}, bf16[128,1024]{1,0:T(8,128)(2,1)}, u32[]{:S(2)}) copy-start(bf16[128,1024]{1,0:T(8,128)(2,1)} %copy-done.27) | copy-start | bytes 786436
  358.9 20.0 %collective-permute-start.28 = (bf16[1,640,256]{2,1,0:T(8,128)(2,1)S(1)}, bf16[1,640,256]{2,1,0:T(8,128)(2,1)S(1)}, u32[]{:S(2)}, u32[]{:S(2)}) collective-permute-start(bf16[1,640,256]{2,1,0:T(8,128)(2,1)S(1)} %get-tuple-element.79), channel_id=1, source_target_pairs={{0,8},{8,16},{16,24},{24,0},{1,9},{9,17},{17,25},{25,1},{2,10},{10... | collective-permute-start | bytes 983048 | tf_op jit(solution)/shard_map/ppermute | solution.py:182
  370.7 24.2 %collective-permute-start.29 = (bf16[1,640,256]{2,1,0:T(8,128)(2,1)S(1)}, bf16[1,640,256]{2,1,0:T(8,128)(2,1)S(1)}, u32[]{:S(2)}, u32[]{:S(2)}) collective-permute-start(bf16[1,640,256]{2,1,0:T(8,128)(2,1)S(1)} %get-tuple-element.81), channel_id=1, source_target_pairs={{0,16},{8,24},{16,0},{24,8},{1,17},{9,25},{17,1},{25,9},{2,18},{10... | collective-permute-start | bytes 983048 | tf_op jit(solution)/shard_map/ppermute | solution.py:182
  370.7 29.2 %collective-permute-start.30 = (bf16[1,640,256]{2,1,0:T(8,128)(2,1)S(1)}, bf16[1,640,256]{2,1,0:T(8,128)(2,1)S(1)}, u32[]{:S(2)}, u32[]{:S(2)}) collective-permute-start(bf16[1,640,256]{2,1,0:T(8,128)(2,1)S(1)} %get-tuple-element.80), channel_id=1, source_target_pairs={{0,24},{8,0},{16,8},{24,16},{1,25},{9,1},{17,9},{25,17},{2,26},{10... | collective-permute-start | bytes 983048 | tf_op jit(solution)/shard_map/ppermute | solution.py:182
  373.3 27.0 %collective-permute-start.16 = (f32[1536]{0:T(1024)S(1)}, f32[1536]{0:T(1024)S(1)}, u32[]{:S(2)}, u32[]{:S(2)}) collective-permute-start(f32[1536]{0:T(1024)S(1)} %get-tuple-element.47), channel_id=1, source_target_pairs={{0,8},{8,16},{16,24},{24,0},{1,9},{9,17},{17,25},{25,1},{2,10},{10... | collective-permute-start | bytes 18440 | tf_op jit(solution)/shard_map/ppermute | solution.py:182
  378.9 21.3 %collective-permute-start.17 = (f32[1536]{0:T(1024)S(1)}, f32[1536]{0:T(1024)S(1)}, u32[]{:S(2)}, u32[]{:S(2)}) collective-permute-start(f32[1536]{0:T(1024)S(1)} %get-tuple-element.49), channel_id=1, source_target_pairs={{0,16},{8,24},{16,0},{24,8},{1,17},{9,25},{17,1},{25,9},{2,18},{10... | collective-permute-start | bytes 18440 | tf_op jit(solution)/shard_map/ppermute | solution.py:182
  394.9 6.4 %collective-permute-start.18 = (f32[1536]{0:T(1024)S(1)}, f32[1536]{0:T(1024)S(1)}, u32[]{:S(2)}, u32[]{:S(2)}) collective-permute-start(f32[1536]{0:T(1024)S(1)} %get-tuple-element.48), channel_id=1, source_target_pairs={{0,24},{8,0},{16,8},{24,16},{1,25},{9,1},{17,9},{25,17},{2,26},{10... | collective-permute-start | bytes 18440 | tf_op jit(solution)/shard_map/ppermute | solution.py:182
  400.1 2.3 collective-permute-start.31
  402.5 16.2 %collective-permute-start.32 = (bf16[2,640,256]{2,1,0:T(8,128)(2,1)S(1)}, bf16[2,640,256]{2,1,0:T(8,128)(2,1)S(1)}, u32[]{:S(2)}, u32[]{:S(2)}) collective-permute-start(bf16[2,640,256]{2,1,0:T(8,128)(2,1)S(1)} %pad_maximum_fusion.12), channel_id=1, source_target_pairs={{0,2},{2,0},{1,3},{3,1},{4,6},{6,4},{5,7},{7,5},{8,10},{10,8},{9,1... | collective-permute-start | bytes 1966088 | tf_op jit(solution)/shard_map/ppermute | solution.py:182
  (22 other events, 59.2 us)
